TPU v7x, 32 devices: a whole 2x2x4 slice. The times are simulated.
32 devices in a mesh: dp: 8 (over z, y), tensor: 4 (over x, core).
Axes of the slice: x: 2, y: 2, z: 4, core: 2. Of those that a mesh axis runs over, the one named last changes fastest.
Arguments:
- tokens: bfloat16 [6144, 1120], P('dp', 'tensor'), may hold values from -6 to 6
- first_gain: float32 [1120], replicated, may hold values from 0.5 to 1.5
- first_shift: float32 [1120], replicated, may hold values from -3 to 3
- triple_weight: bfloat16 [1120, 3, 1120], P(None, None, 'tensor'), may hold values from -0.1875 to 0.1875
- triple_bias: float32 [2, 1120], P(None, 'tensor'), may hold values from -3 to 3
- output_weight: bfloat16 [1120, 1120], P('tensor'), may hold values from -0.5 to 0.5
- output_bias: float32 [1120], replicated, may hold values from -3 to 3
- second_gain: float32 [1120], replicated, may hold values from 0.5 to 1.5
- second_shift: float32 [1120], replicated, may hold values from -3 to 3
- up_weight: bfloat16 [1120, 4480], P(None, 'tensor'), may hold values from -0.1875 to 0.1875
- up_bias: float32 [4480], P('tensor'), may hold values from -3 to 3
- down_weight: bfloat16 [4480, 1120], P('tensor'), may hold values from -0.09375 to 0.09375
- down_bias: float32 [1120], replicated, may hold values from -3 to 3
- cotangent: bfloat16 [6144, 1120], P('dp', 'tensor'), may hold values from -6 to 6
- lengths: int32 [16], P('dp'), may hold values from 96 to 384
Outputs:
- layer_out: bfloat16 [6144, 1120], P('dp', 'tensor')
- input_grad: bfloat16 [6144, 1120], P('dp', 'tensor')
- first_gain_grad: float32 [1120], replicated
- first_shift_grad: float32 [1120], replicated
- triple_weight_grad: float32 [1120, 3, 1120], P(None, None, 'tensor')
- triple_bias_grad: float32 [2, 1120], P(None, 'tensor')
- output_weight_grad: float32 [1120, 1120], P('tensor')
- output_bias_grad: float32 [1120], replicated
- second_gain_grad: float32 [1120], replicated
- second_shift_grad: float32 [1120], replicated
- up_weight_grad: float32 [1120, 4480], P(None, 'tensor')
- up_bias_grad: float32 [4480], P('tensor')
- down_weight_grad: float32 [4480, 1120], P('tensor')
- down_bias_grad: float32 [1120], replicated
All inputs are finite; a program needn't handle non-finite values.
Results may differ from a plain program's by a relative error of at most 0.019.
Values may be sent and summed in bfloat16 or wider, within the bound.
No kernel may reach another device: no remote copies, remote signals or barrier semaphores. Data moves between devices by JAX's collectives and lax.ppermute only.
A program may use at most 128 MiB of HBM per device.

v0:
```python
import functools

import jax
import jax.numpy as jnp
from jax import lax
from jax.experimental import pallas as pl
from jax.experimental.pallas import tpu as pltpu
from jax.sharding import PartitionSpec as P

HEAD_DIM = 56
CELL_LEN = 384
LANES = 128
WIDE = 256
epsilon = 1e-05
CURVE = 0.7978845608028654
CUBIC = 0.044715
bf16 = jnp.bfloat16
f32 = jnp.float32
MIB = 1024 * 1024
SMALL = 6


def dot_nn(left, right):
    return lax.dot_general(left, right, (((1,), (0,)), ((), ())), preferred_element_type=f32)


def dot_nt(left, right):
    return lax.dot_general(left, right, (((1,), (1,)), ((), ())), preferred_element_type=f32)


def dot_tn(left, right):
    return lax.dot_general(left, right, (((0,), (0,)), ((), ())), preferred_element_type=f32)


def struct(shape, dtype=bf16):
    return jax.ShapeDtypeStruct(shape, dtype)


CHAIN = []


def in_turn(arguments, first):
    if CHAIN:
        held = lax.optimization_barrier((arguments[first], CHAIN[0]))[0]
        arguments = (*arguments[:first], held, *arguments[first + 1 :])
    return arguments


def call(kernel, name, out_shape, flops, *arguments, scratch=(), scalars=0, limit=12, transcendentals=0, far_in=(), far_out=()):
    inputs = [pl.ANY if place in far_in else pltpu.VMEM for place in range(len(arguments) - scalars)]
    outputs = [pl.ANY if place in far_out else pltpu.VMEM for place in range(len(out_shape))]
    results = pl.pallas_call(
        kernel,
        in_specs=[pl.BlockSpec(memory_space=space) for space in [pltpu.SMEM] * scalars + inputs],
        out_specs=[pl.BlockSpec(memory_space=space) for space in outputs],
        out_shape=out_shape,
        scratch_shapes=scratch,
        compiler_params=pltpu.CompilerParams(vmem_limit_bytes=limit * MIB),
        name=name,
    )(*in_turn(arguments, scalars))
    CHAIN[:] = results[:1]
    return results


def loop(count, step):
    def wrapped(index, carry):
        step(index)
        return carry

    lax.fori_loop(0, count, wrapped, 0)


def by_rows(rows, step):
    whole = rows // 64

    def block(index):
        step(pl.multiple_of(index * 64, 64), 64)

    loop(whole, block)
    if rows % 64:
        step(64 * whole, rows % 64)


def lanes_at(index, size):
    return pl.ds(pl.multiple_of(index * size, size), size)


def start_copies(pairs, sems, first=0):
    copies = [
        pltpu.make_async_copy(source, target, sems.at[first + place])
        for place, (source, target) in enumerate(pairs)
    ]
    for copy in copies:
        copy.start()
    return copies


def wait_for(copies):
    for copy in copies:
        copy.wait()


def place_pieces(place, refs, target):
    share = refs[0].shape[0]
    for offset, ref in enumerate(refs):
        base = lax.bitwise_xor(place, offset) * share

        def step(start, size):
            value = ref[pl.ds(start, size), :].astype(target.dtype)
            target[pl.ds(pl.multiple_of(base + start, 8), size), :] = value

        by_rows(share, step)


def norm_columns(field, gain, shift):
    center = field - jnp.mean(field, 0, keepdims=True)
    spread = jnp.mean(center * center, 0, keepdims=True)
    return center * lax.rsqrt(spread + epsilon) * gain + shift


def front_kernel(
    place_ref, length_ref, own, near, far, both, weight_far, columns, bias,
    rows_far, normed_far, triple_far, probs_far, context_out,
    field, pieces, weight, rows_out, normed_out, triple_out, probs_out, sems,
):
    share = context_out.shape[0]
    heads = share // HEAD_DIM
    tokens = rows_out.shape[1]
    arrived = [pieces.at[offset] for offset in range(4)]
    copies = start_copies([*zip((own, near, far, both), arrived), (weight_far, weight)], sems)
    wait_for(copies[:4])
    place_pieces(place_ref[0], arrived, field)

    def norm_step(index):
        lanes = lanes_at(index, LANES)
        value = field[:, lanes]
        rows_out[:, lanes] = value.astype(bf16)
        normed_out[:, lanes] = norm_columns(value, columns[:, 0:1], columns[:, 1:2]).astype(bf16)

    loop(tokens // LANES, norm_step)
    copies[4].wait()
    leaving = start_copies([(rows_out, rows_far), (normed_out, normed_far)], sems, 5)

    def project_step(index):
        lanes = lanes_at(index, WIDE)
        triple_out[:, lanes] = (dot_nn(weight[...], normed_out[:, lanes]) + bias[...]).astype(bf16)

    loop(tokens // WIDE, project_step)
    leaving += start_copies([(triple_out, triple_far)], sems, 7)
    factor = HEAD_DIM ** (-0.5)

    def cell_step(cell):
        length = length_ref[cell]
        for head in range(heads):
            start = HEAD_DIM * head
            for block in range(CELL_LEN // LANES):
                span = LANES * (block + 1)
                base = pl.multiple_of(cell * CELL_LEN, LANES)
                here = pl.ds(pl.multiple_of(base + LANES * block, LANES), LANES)
                queries = triple_out[start : start + HEAD_DIM, here]
                keys = triple_out[share + start : share + start + HEAD_DIM, pl.ds(base, span)]
                values = triple_out[2 * share + start : 2 * share + start + HEAD_DIM, pl.ds(base, span)]
                scores = dot_tn(keys, queries) * factor
                key_place = lax.broadcasted_iota(jnp.int32, (span, LANES), 0)
                query_place = lax.broadcasted_iota(jnp.int32, (span, LANES), 1) + LANES * block
                allowed = (key_place <= query_place) & (key_place < length)
                masked = jnp.where(allowed, scores, -1e30)
                expo = jnp.exp(masked - jnp.max(masked, 0, keepdims=True))
                probs = (expo / jnp.sum(expo, 0, keepdims=True)).astype(bf16)
                probs_out[cell, head, :span, LANES * block : span] = probs
                context_out[start : start + HEAD_DIM, here] = dot_nn(values, probs).astype(bf16)
        pltpu.make_async_copy(probs_out.at[cell], probs_far.at[cell], sems.at[8 + cell]).start()

    loop(tokens // CELL_LEN, cell_step)
    for cell in range(tokens // CELL_LEN):
        pltpu.make_async_copy(probs_out.at[cell], probs_far.at[cell], sems.at[8 + cell]).wait()
    wait_for(leaving)


def front_call(place, lengths, pieces, columns, weight, bias):
    share, tokens = pieces[0].shape
    width = weight.shape[1]
    heads = share // HEAD_DIM
    cells = tokens // CELL_LEN
    pairs = cells * heads * CELL_LEN * CELL_LEN
    return call(
        front_kernel,
        "front",
        [
            struct((width, tokens)),
            struct((width, tokens)),
            struct((3 * share, tokens)),
            struct((cells, heads, CELL_LEN, CELL_LEN)),
            struct((share, tokens)),
        ],
        tokens * width * share * 6 + pairs * HEAD_DIM * 4,
        place, lengths, *pieces, weight, columns, bias,
        scratch=[
            pltpu.VMEM((width, tokens), f32),
            pltpu.VMEM((4, share, tokens), bf16),
            pltpu.VMEM(weight.shape, bf16),
            pltpu.VMEM((width, tokens), bf16),
            pltpu.VMEM((width, tokens), bf16),
            pltpu.VMEM((3 * share, tokens), bf16),
            pltpu.VMEM((cells, heads, CELL_LEN, CELL_LEN), bf16),
            pltpu.SemaphoreType.DMA((8 + cells,)),
        ],
        scalars=2,
        limit=60,
        far_in=range(5),
        far_out=range(4),
        transcendentals=pairs,
    )


def gate_parts(value):
    square = value * value
    bend = jnp.tanh(CURVE * (value + CUBIC * square * value))
    upper = 0.5 * (1.0 + bend)
    slope = upper + 0.5 * value * (1.0 - bend * bend) * CURVE * (1.0 + 3.0 * CUBIC * square)
    return value * upper, slope


def middle_kernel(
    own, near, far, both, own_weight, near_weight, far_weight, both_weight, rows_far, up_far, columns,
    resid_far, normed_far, hidden_out, slope_out,
    field, weight, pieces, weights, rows_ref, up, resid_out, normed_out, sems,
):
    tokens = resid_out.shape[1]
    share = own.shape[0]
    sources = own, near, far, both, own_weight, near_weight, far_weight, both_weight
    targets = [pieces.at[place] for place in range(4)] + [weights.at[place] for place in range(4)]
    copies = start_copies([*zip(sources, targets), (rows_far, rows_ref), (up_far, up)], sems)
    wait_for(copies[:8])
    place_pieces(0, [pieces.at[place] for place in range(4)], field)
    for place in range(4):
        weight[:, share * place : share * (place + 1)] = weights[place]
    wait_for(copies[8:])

    def leaving(index):
        lanes = lanes_at(index, WIDE)
        resid_copy = pltpu.make_async_copy(
            resid_out.at[:, lanes], resid_far.at[:, lanes], sems.at[10 + 2 * index]
        )
        normed_copy = pltpu.make_async_copy(
            normed_out.at[:, lanes], normed_far.at[:, lanes], sems.at[11 + 2 * index]
        )
        return resid_copy, normed_copy

    def step(index):
        lanes = lanes_at(index, WIDE)
        added = dot_nn(weight[...], field[:, lanes].astype(bf16))
        resid = rows_ref[:, lanes].astype(f32) + added + columns[:, 2:3]
        resid_out[:, lanes] = resid
        normed = norm_columns(resid, columns[:, 3:4], columns[:, 4:5]).astype(bf16)
        normed_out[:, lanes] = normed
        hidden, slope = gate_parts(dot_nn(up[...], normed) + columns[:, 5:6])
        hidden_out[:, lanes] = hidden.astype(bf16)
        slope_out[:, lanes] = slope
        for copy in leaving(index):
            copy.start()

    loop(tokens // WIDE, step)
    for index in range(tokens // WIDE):
        wait_for(leaving(index))


def middle_call(pieces, weights, rows_all, columns, up):
    width, tokens = rows_all.shape
    hidden = up.shape[0]
    return call(
        middle_kernel,
        "middle",
        [
            struct((width, tokens), f32),
            struct((width, tokens)),
            struct((hidden, tokens)),
            struct((hidden, tokens), f32),
        ],
        tokens * width * (width + hidden) * 2,
        *pieces, *weights, rows_all, up, columns,
        scratch=[
            pltpu.VMEM((width, tokens), f32),
            pltpu.VMEM((width, width), bf16),
            pltpu.VMEM((4, *pieces[0].shape), bf16),
            pltpu.VMEM((4, *weights[0].shape), bf16),
            pltpu.VMEM((width, tokens), bf16),
            pltpu.VMEM(up.shape, bf16),
            pltpu.VMEM((width, tokens), f32),
            pltpu.VMEM((width, tokens), bf16),
            pltpu.SemaphoreType.DMA((10 + 2 * (tokens // WIDE),)),
        ],
        limit=53,
        far_in=range(10),
        far_out=range(2),
        transcendentals=tokens * hidden,
    )


def spread_kernel(place_ref, own, near, far, both, rows_out, sums_out, field):
    place_pieces(place_ref[0], (own, near, far, both), field)
    rows_out[...] = field[...].astype(bf16)
    sums_out[...] = jnp.sum(field[...], 1, keepdims=True)


def spread_call(place, pieces):
    share, tokens = pieces[0].shape
    return call(
        spread_kernel,
        "spread",
        [struct((4 * share, tokens)), struct((4 * share, 1), f32)],
        4 * share * tokens,
        place, *pieces,
        scratch=[pltpu.VMEM((4 * share, tokens), f32)],
        scalars=1,
    )


def store_halves(bit, value, lanes, keep_out, send_out):
    half = keep_out.shape[0]

    @pl.when(bit == 0)
    def _():
        keep_out[:, lanes] = value[:half]
        send_out[:, lanes] = value[half:]

    @pl.when(bit != 0)
    def _():
        keep_out[:, lanes] = value[half:]
        send_out[:, lanes] = value[:half]


def turn_kernel(
    place_ref, cotangent, slope, down, up, pre_out, keep_out, send_out, sums_out,
):
    tokens = cotangent.shape[1]
    core = lax.rem(place_ref[0], 2)
    sums_out[...] = jnp.zeros_like(sums_out)

    def step(index):
        lanes = lanes_at(index, WIDE)
        pre = dot_nn(down[...], cotangent[:, lanes]) * slope[:, lanes]
        sums_out[...] += jnp.sum(pre, 1, keepdims=True)
        low = pre.astype(bf16)
        pre_out[:, lanes] = low
        store_halves(core, dot_nn(up[...], low).astype(bf16), lanes, keep_out, send_out)

    loop(tokens // WIDE, step)


def turn_call(place, cotangent, slope, down, up):
    width, tokens = cotangent.shape
    hidden = up.shape[1]
    return call(
        turn_kernel,
        "turn",
        [
            struct((hidden, tokens)),
            struct((width // 2, tokens)),
            struct((width // 2, tokens)),
            struct((hidden, 1), f32),
        ],
        tokens * width * hidden * 4,
        place, cotangent, slope, down, up,
        scalars=1,
    )


def norm_back(field, grad, gain):
    center = field - jnp.mean(field, 0, keepdims=True)
    inverse = lax.rsqrt(jnp.mean(center * center, 0, keepdims=True) + epsilon)
    normed = center * inverse
    scaled = grad * gain
    inner = jnp.mean(scaled * normed, 0, keepdims=True)
    back = inverse * (scaled - jnp.mean(scaled, 0, keepdims=True) - normed * inner)
    return normed, back


def add_parts(left, right):
    return (left.astype(f32) + right.astype(f32)).astype(bf16)


def back_kernel(
    place_ref, mine, other, resid, cotangent, columns, out_weight, triple, probs_ref, weight,
    dh_out, low_out, triple_out, keep_out, send_out, sums_out, bias_out,
    grad, context_grad, gain_sum, shift_sum, total_sum,
):
    share = out_weight.shape[0]
    width, tokens = resid.shape
    half = width // 2
    heads = share // HEAD_DIM
    factor = HEAD_DIM ** (-0.5)
    core = lax.rem(place_ref[0], 2)
    place_pieces(core, (mine, other), grad)
    for item in (gain_sum, shift_sum, total_sum, bias_out):
        item[...] = jnp.zeros_like(item)

    def norm_step(index):
        lanes = lanes_at(index, LANES)
        upper = grad[:, lanes]
        normed, back = norm_back(resid[:, lanes], upper, columns[:, 3:4])
        total = cotangent[:, lanes].astype(f32) + back
        dh_out[:, lanes] = total
        low_out[:, lanes] = total.astype(bf16)
        gain_sum[...] += upper * normed
        shift_sum[...] += upper
        total_sum[...] += total

    loop(tokens // LANES, norm_step)
    sums_out[:, 0:1] = jnp.sum(gain_sum[...], 1, keepdims=True)
    sums_out[:, 1:2] = jnp.sum(shift_sum[...], 1, keepdims=True)
    sums_out[:, 2:3] = jnp.sum(total_sum[...], 1, keepdims=True)

    def context_step(index):
        lanes = lanes_at(index, WIDE)
        context_grad[:, lanes] = dot_nn(out_weight[...], low_out[:, lanes]).astype(bf16)

    loop(tokens // WIDE, context_step)
    blocks = CELL_LEN // LANES

    def cell_step(cell):
        base = pl.multiple_of(cell * CELL_LEN, LANES)
        for head in range(heads):
            start = HEAD_DIM * head
            query_rows = slice(start, start + HEAD_DIM)
            key_rows = slice(share + start, share + start + HEAD_DIM)
            value_rows = slice(2 * share + start, 2 * share + start + HEAD_DIM)
            key_grads = [None] * blocks
            value_grads = [None] * blocks
            query_sum = jnp.zeros((HEAD_DIM, 1), f32)
            value_sum = jnp.zeros((HEAD_DIM, 1), f32)
            for block in range(blocks):
                span = LANES * (block + 1)
                here = pl.ds(pl.multiple_of(base + LANES * block, LANES), LANES)
                queries = triple[query_rows, here]
                keys = triple[key_rows, pl.ds(base, span)]
                values = triple[value_rows, pl.ds(base, span)]
                low = context_grad[query_rows, here]
                probs_low = probs_ref[cell, head, :span, LANES * block : span]
                probs = probs_low.astype(f32)
                prob_grad = dot_tn(values, low)
                inner = jnp.sum(prob_grad * probs, 0, keepdims=True)
                score = (probs * (prob_grad - inner) * factor).astype(bf16)
                query_grad = dot_nn(keys, score)
                query_sum += jnp.sum(query_grad, 1, keepdims=True)
                triple_out[query_rows, here] = query_grad.astype(bf16)
                key_part = dot_nt(queries, score)
                value_part = dot_nt(low, probs_low)
                for place in range(block + 1):
                    lanes = slice(LANES * place, LANES * (place + 1))
                    if key_grads[place] is None:
                        key_grads[place] = key_part[:, lanes]
                        value_grads[place] = value_part[:, lanes]
                    else:
                        key_grads[place] += key_part[:, lanes]
                        value_grads[place] += value_part[:, lanes]
            for block in range(blocks):
                here = pl.ds(pl.multiple_of(base + LANES * block, LANES), LANES)
                triple_out[key_rows, here] = key_grads[block].astype(bf16)
                triple_out[value_rows, here] = value_grads[block].astype(bf16)
                value_sum += jnp.sum(value_grads[block], 1, keepdims=True)
            bias_out[query_rows, 0:1] += query_sum
            bias_out[query_rows, 1:2] += value_sum

    loop(tokens // CELL_LEN, cell_step)

    def part_step(index):
        lanes = lanes_at(index, WIDE)
        part = dot_nn(weight[...], triple_out[:, lanes]).astype(bf16)
        store_halves(core, part, lanes, keep_out, send_out)

    loop(tokens // WIDE, part_step)


def back_call(place, mine, other, resid, cotangent, columns, out_weight, triple, probs, weight):
    width, tokens = resid.shape
    share = out_weight.shape[0]
    cells, heads = probs.shape[:2]
    pairs = cells * heads * CELL_LEN * CELL_LEN
    return call(
        back_kernel,
        "back",
        [
            struct((width, tokens), f32),
            struct((width, tokens)),
            struct((3 * share, tokens)),
            struct((width // 2, tokens)),
            struct((width // 2, tokens)),
            struct((width, 8), f32),
            struct((share, 8), f32),
        ],
        tokens * width * share * 8 + pairs * HEAD_DIM * 8,
        place, mine, other, resid, cotangent, columns, out_weight, triple, probs, weight,
        scratch=[pltpu.VMEM((width, tokens), f32), pltpu.VMEM((share, tokens), bf16)]
        + [pltpu.VMEM((width, LANES), f32)] * 3,
        scalars=1,
    )


def last_kernel(
    place_ref, mine, other, rows_ref, dh, columns, cotangent_sums, pre_sums, back_sums, bias_sums,
    out, sums_out, grad, gain_sum, shift_sum, field,
):
    share, tokens = out.shape
    width = rows_ref.shape[0]
    half = width // 2
    place = place_ref[0]
    core = lax.rem(place, 2)
    place_pieces(core, (mine, other), grad)
    gain_sum[...] = jnp.zeros_like(gain_sum)
    shift_sum[...] = jnp.zeros_like(shift_sum)

    def norm_step(index):
        lanes = lanes_at(index, LANES)
        upper = grad[:, lanes]
        normed, back = norm_back(rows_ref[:, lanes].astype(f32), upper, columns[:, 0:1])
        field[...] = dh[:, lanes] + back
        out[:, lanes] = field[pl.ds(pl.multiple_of(place * share, 8), share), :].astype(bf16)
        gain_sum[...] += upper * normed
        shift_sum[...] += upper

    loop(tokens // LANES, norm_step)
    field[:, 0:1] = jnp.sum(gain_sum[...], 1, keepdims=True)
    field[:, 1:2] = jnp.sum(shift_sum[...], 1, keepdims=True)
    field[:, 2:3] = cotangent_sums[...]
    field[:, 3:4] = pre_sums[...]
    field[:, 4:7] = back_sums[:, 0:3]
    field[0:share, 7:9] = bias_sums[:, 0:2]
    sums_out[...] = field[...].T[0:16, :]


def last_call(place, mine, other, rows_all, dh, columns, *sums):
    width, tokens = rows_all.shape
    return call(
        last_kernel,
        "last",
        [struct((width // 4, tokens)), struct((16, width), f32)],
        width * tokens * 12,
        place, mine, other, rows_all, dh, columns, *sums,
        scratch=[pltpu.VMEM((width, tokens), f32)] + [pltpu.VMEM((width, LANES), f32)] * 3,
        scalars=1,
    )


def add_kernel(left, right, out):
    def step(start, size):
        rows = pl.ds(start, size)
        out[rows, :] = add_parts(left[rows, :], right[rows, :])

    by_rows(out.shape[0], step)


def add_call(left, right):
    return call(add_kernel, "add", [struct(left.shape)], left.size, left, right, limit=SMALL)[0]


def add_wide_kernel(left, right, out):
    out[...] = left[...] + right[...]


def add_wide_call(left, right):
    return call(add_wide_kernel, "add_wide", [struct(left.shape, f32)], left.size, left, right, limit=SMALL)[0]


def down_kernel(place_ref, hidden, down, keep_out, send_out):
    tokens = hidden.shape[1]
    share = keep_out.shape[0] // 2
    core = lax.rem(place_ref[0], 2)

    def step(index):
        lanes = lanes_at(index, WIDE)
        part = dot_nn(down[...], hidden[:, lanes]).astype(bf16)
        for chip in range(2):
            rows = slice(share * chip, share * (chip + 1))
            low = part[2 * share * chip : 2 * share * chip + share]
            high = part[2 * share * chip + share : 2 * share * (chip + 1)]

            @pl.when(core == 0)
            def _():
                keep_out[rows, lanes] = low
                send_out[rows, lanes] = high

            @pl.when(core != 0)
            def _():
                keep_out[rows, lanes] = high
                send_out[rows, lanes] = low

    loop(tokens // WIDE, step)


def down_call(place, hidden, down):
    width, inner = down.shape
    tokens = hidden.shape[1]
    return call(
        down_kernel,
        "down",
        [struct((width // 2, tokens))] * 2,
        tokens * width * inner * 2,
        place, hidden, down,
        scalars=1,
    )


def down_add_kernel(place_ref, keep, got, keep_out, send_out, field):
    share = keep_out.shape[0]
    chip = lax.div(place_ref[0], 2)
    field[...] = keep[...].astype(f32) + got[...].astype(f32)
    keep_out[...] = field[pl.ds(pl.multiple_of(chip * share, 8), share), :].astype(bf16)
    send_out[...] = field[pl.ds(pl.multiple_of((1 - chip) * share, 8), share), :].astype(bf16)


def down_add_call(place, keep, got):
    rows, tokens = keep.shape
    return call(
        down_add_kernel,
        "down_add",
        [struct((rows // 2, tokens))] * 2,
        keep.size,
        place, keep, got,
        scratch=[pltpu.VMEM(keep.shape, f32)],
        scalars=1,
    )


def layer_out_kernel(place_ref, keep, got, resid, columns, out):
    share = out.shape[0]
    rows = pl.ds(pl.multiple_of(place_ref[0] * share, 8), share)
    total = keep[...].astype(f32) + got[...].astype(f32)
    out[...] = (resid[rows, :] + total + columns[rows, 6:7]).astype(bf16)


def layer_out_call(place, keep, got, resid, columns):
    return call(
        layer_out_kernel,
        "layer_out",
        [struct(keep.shape)],
        keep.size,
        place, keep, got, resid, columns,
        scalars=1,
    )[0]


def grad_kernel(ranges, place_ref, *refs):
    pairs, (keep_out, send_out) = refs[:-2], refs[-2:]
    side = lax.rem(place_ref[0], 2)
    width = keep_out.shape[1]

    def step(lanes):
        parts = []
        for left, right, (low, high) in zip(pairs[0::2], pairs[1::2], ranges):
            parts.append(dot_nt(left[low:high, :], right[lanes, :]).astype(bf16))
        value = parts[0] if len(parts) == 1 else jnp.concatenate(parts, 0)
        store_halves(side, value, lanes, keep_out, send_out)

    loop(width // WIDE, lambda index: step(lanes_at(index, WIDE)))
    if width % WIDE:
        step(slice(width - width % WIDE, width))


def grad_call(dp_place, ranges, *pairs):
    rows = sum(high - low for low, high in ranges)
    tokens = pairs[0].shape[1]
    width = pairs[1].shape[0]
    return call(
        functools.partial(grad_kernel, ranges),
        "grad",
        [struct((rows // 2, width)), struct((rows // 2, width))],
        2 * rows * tokens * width,
        dp_place, *pairs,
        scalars=1,
    )


def settle_kernel(dp_ref, mine, got, out):
    def copy_from(ref):
        def step(start, size):
            rows = pl.ds(start, size)
            out[rows, :] = ref[rows, :]

        by_rows(out.shape[0], step)

    pl.when(dp_ref[2] == 1)(lambda: copy_from(got))
    pl.when(dp_ref[2] == 0)(lambda: copy_from(mine))


def settle_call(dp, mine, got):
    return call(settle_kernel, "settle", [struct(mine.shape)], mine.size, dp, mine, got, scalars=1, limit=SMALL)[0]


def final_kernel(count, dp_ref, *refs):
    side = lax.rem(dp_ref[0], 2)
    outs = refs[2 * count :]

    def put(start, ref):
        done = 0
        rows = ref.shape[0]
        for out in outs:
            size = out.shape[0]
            low, high = max(start, done), min(start + rows, done + size)
            if low < high:

                def step(begin, count):
                    value = ref[pl.ds(low - start + begin, count), :].astype(f32)
                    out[pl.ds(low - done + begin, count), :] = value

                by_rows(high - low, step)
            done += size

    base = 0
    for place in range(count):
        mine, got = refs[2 * place : 2 * place + 2]
        half = mine.shape[0]

        @pl.when(side == 0)
        def _():
            put(base, mine)
            put(base + half, got)

        @pl.when(side != 0)
        def _():
            put(base, got)
            put(base + half, mine)

        base += 2 * half


def final_call(dp, parts, sizes):
    width = parts[0].shape[1]
    return call(
        functools.partial(final_kernel, len(parts) // 2),
        "final",
        [struct((size, width), f32) for size in sizes],
        sum(sizes) * width,
        dp, *parts,
        scalars=1,
        limit=SMALL,
    )


def swap_core(value):
    return lax.ppermute(value, "tensor", [(place, place ^ 1) for place in range(4)])


def swap_chip(value):
    return lax.ppermute(value, "tensor", [(place, place ^ 2) for place in range(4)])


def after(value, *others):
    return lax.optimization_barrier((value, *others))[0]


def all_pieces(share):
    far = swap_chip(share)
    return share, swap_core(share), far, swap_core(far)


def ordered(bit, mine, other, axis):
    low = jnp.where(bit == 0, mine, other)
    high = jnp.where(bit == 0, other, mine)
    return jnp.concatenate([low, high], axis)


def line_pairs(pairs):
    return [(2 * source + side, 2 * target + side) for source, target in pairs for side in (0, 1)]


INWARD = line_pairs([(0, 1), (3, 2)])
MIDDLE = line_pairs([(1, 2), (2, 1)])
OUTWARD = line_pairs([(1, 0), (2, 3)])
ACROSS = [(place, place ^ 1) for place in range(8)]
ACROSS_MIDDLE = [(2, 3), (3, 2), (4, 5), (5, 4)]


def hop(value, pairs):
    return lax.ppermute(value, "dp", pairs)


STAGES = (ACROSS, INWARD, MIDDLE, OUTWARD, ACROSS)


class CellSum:
    def __init__(self, groups, dp, parts):
        self.groups, self.dp = groups, dp
        self.mine, self.got = parts
        self.stage = -1

    def step(self):
        self.stage += 1
        if self.groups != 8:
            return
        send = self.got
        if self.stage == 4:
            send = self.mine = settle_call(self.dp, self.mine, self.got)
        elif self.stage > 0:
            send = self.mine = add_call(self.mine, self.got)
        self.got = hop(send, STAGES[self.stage])

    def plain(self):
        value = ordered(self.dp[0] % 2, self.mine, self.got, 0)
        return lax.psum(value, "dp").astype(f32)


def finish(sums, sizes):
    if sums[0].groups == 8:
        return final_call(sums[0].dp, [piece for item in sums for piece in (item.mine, item.got)], sizes)
    value = jnp.concatenate([item.plain() for item in sums], 0)
    ends = [sum(sizes[: place + 1]) for place in range(len(sizes))]
    return [value[end - size : end] for end, size in zip(ends, sizes)]


def end_round(sums, *values):
    held = lax.optimization_barrier((*[item.got for item in sums], *values))
    for item, got in zip(sums, held):
        item.got = got
    return held[len(sums) :]


def body(
    groups,
    tokens,
    first_gain,
    first_shift,
    triple_weight,
    triple_bias,
    output_weight,
    output_bias,
    second_gain,
    second_shift,
    up_weight,
    up_bias,
    down_weight,
    down_bias,
    cotangent,
    lengths,
):
    share = tokens.shape[1]
    width = triple_weight.shape[0]
    index = lax.axis_index("tensor").astype(jnp.int32)
    core, chip = index % 2, index // 2
    place = index.reshape(1)
    row = lax.axis_index("dp").astype(jnp.int32)
    at_end = ((row < 2) | (row >= groups - 2)).astype(jnp.int32)
    dp = jnp.stack([row, jnp.int32(groups // 2), at_end])
    CHAIN.clear()
    fence = lambda *values: lax.optimization_barrier(values)
    token_own, grad_own = tokens.T, cotangent.T
    token_far, token_near = swap_chip(token_own), swap_core(token_own)
    grad_near, weight_near = swap_core(grad_own), swap_core(output_weight)
    triple_t = triple_weight.transpose(1, 2, 0).reshape(3 * share, width)
    bias_flat = jnp.concatenate([triple_bias[0], jnp.zeros((share,), f32), triple_bias[1]])[:, None]
    columns = jnp.stack(
        [first_gain, first_shift, output_bias, second_gain, second_shift, up_bias, down_bias], 1
    )
    up_t, triple_plain = up_weight.T, triple_t.T
    token_far, token_near, up_t, triple_plain, columns, bias_flat, out_weight = fence(
        token_far, token_near, up_t, triple_plain, columns, bias_flat, output_weight
    )
    token_both = swap_core(token_far)
    weight_far = swap_chip(out_weight)
    own_t = out_weight.T
    token_both, own_t = fence(token_both, own_t)
    rows_all, first_normed, triple, probs, context = front_call(
        place, lengths, (token_own, token_near, token_far, token_both), columns, triple_t, bias_flat
    )
    context_far, context_near = swap_chip(context), swap_core(context)
    weight_far, weight_near, down_plain, _ = fence(weight_far, weight_near, down_weight, context)
    weight_both = swap_core(weight_far)
    weights = own_t, weight_near.T, weight_far.T, weight_both.T
    down_t = down_plain.T
    context_far, context_near, down_t, grad_own, *weights = fence(
        context_far, context_near, down_t, grad_own, *weights
    )
    context_both = swap_core(context_far)
    grad_far = swap_chip(grad_own)
    resid, second_normed, hidden, slope = middle_call(
        (context, context_near, context_far, context_both), weights, rows_all, columns, up_t
    )
    grad_far, _ = fence(grad_far, second_normed)
    grad_both = swap_core(grad_far)
    grad_rows, cotangent_sums = spread_call(place, (grad_own, grad_near, grad_far, grad_both))
    half = width // 2

    def cell_sum(ranges, *pairs):
        return CellSum(groups, dp, grad_call(dp, ranges, *pairs))

    down_low = cell_sum([(0, half)], hidden, grad_rows)
    down_low.step()
    pre_low, keep, send, pre_sums = turn_call(place, grad_rows, slope, down_weight, up_weight)
    keep, send = end_round([down_low], keep, send)
    near = swap_core(send)
    down_low.step()
    down_keep, down_send = down_call(place, hidden, down_t)
    near = add_call(keep, near)
    far = swap_chip(near)
    down_high = cell_sum([(half, width)], hidden, grad_rows)
    down_high.step()
    down_got = swap_core(down_send)
    up_low = cell_sum([(0, half)], second_normed, pre_low)
    up_high = cell_sum([(half, width)], second_normed, pre_low)
    far, down_got, near, _ = end_round([down_low, down_high], far, down_got, near, up_high.mine)
    mine = add_call(near, far)
    other = swap_core(mine)
    for item in (down_high, down_low, up_low, up_high):
        item.step()
    dh, low, triple_low, keep, send, back_sums, bias_sums = back_call(
        place, mine, other, resid, grad_rows, columns, output_weight, triple, probs, triple_plain
    )
    keep, send = end_round([down_low, down_high, up_low, up_high], keep, send)
    near = swap_core(send)
    early = cell_sum([(0, 2 * share)], triple_low, first_normed)
    near = add_call(keep, near)
    far = swap_chip(near)
    for item in (up_low, down_high, down_low, early):
        item.step()
    late = cell_sum([(2 * share, 3 * share), (0, share)], triple_low, first_normed, context, low)
    far, near, _ = end_round([early, down_low, down_high, up_low, up_high], far, near, late.mine)
    mine = add_call(near, far)
    other = swap_core(mine)
    for item in (early, up_low, down_high, late):
        item.step()
    down_keep, down_send = down_add_call(place, down_keep, down_got)
    down_got = swap_chip(down_send)
    input_grad, small = last_call(
        place, mine, other, rows_all, dh, columns, cotangent_sums, pre_sums, back_sums, bias_sums
    )
    small, down_got = end_round([down_low, down_high, up_low, up_high, early, late], small, down_got)
    shifts = (1, 4, 2)
    if groups != 8:
        small = lax.psum(small, "dp")
    rounds = [
        (late, early, up_low, down_low),
        (up_high, late, early, down_high),
        (up_high, late, up_low),
        (early, up_high),
        (late, up_high),
    ]
    for place_in, items in enumerate(rounds):
        if groups == 8 and place_in < 3:
            got = hop(small, [(spot, spot ^ shifts[place_in]) for spot in range(8)])
        for item in items:
            item.step()
        if place_in == 2:
            down_grad = finish([down_low, down_high], [width])[0]
        if place_in == 0:
            layer_out = layer_out_call(place, down_keep, down_got, resid, columns)
        if groups == 8 and place_in < 3:
            (got,) = end_round(list(items), got)
            small = add_wide_call(small, got)
        else:
            end_round(list(items))
    up_grad = finish([up_low, up_high], [width])[0]
    triple_grad, output_grad = finish([early, late], [3 * share, share])
    triple_grad = triple_grad.reshape(3, share, width).transpose(2, 0, 1)
    return (
        layer_out.T,
        input_grad.T,
        small[0],
        small[1],
        triple_grad,
        small[7:9, :share],
        output_grad,
        small[6],
        small[4],
        small[5],
        up_grad,
        small[3],
        down_grad,
        small[2],
    )


def solution(mesh):
    placed = (
        P("dp", "tensor"),
        P(),
        P(),
        P(None, None, "tensor"),
        P(None, "tensor"),
        P("tensor", None),
        P(),
        P(),
        P(),
        P(None, "tensor"),
        P("tensor"),
        P("tensor", None),
        P(),
        P("dp", "tensor"),
        P("dp"),
    )
    return jax.shard_map(
        functools.partial(body, mesh.shape["dp"]),
        mesh=mesh,
        in_specs=placed,
        out_specs=(
            P("dp", "tensor"),
            P("dp", "tensor"),
            P(),
            P(),
            P(None, None, "tensor"),
            P(None, "tensor"),
            P("tensor", None),
            P(),
            P(),
            P(),
            P(None, "tensor"),
            P("tensor"),
            P("tensor", None),
            P(),
        ),
        check_vma=False,
    )
```

profile of v0, /device:TPU:0, one launch (start us, length us, event | category | flops | bytes accessed | tf_op | source)
XLA Modules:
  0.0 317.7 jit_solution(2426397929160925811)
XLA Ops:
  0.7 3.0 collective-permute-start
  5.1 4.0 %copy.51 = bf16[840,1120]{0,1:T(8,128)(2,1)} copy(bf16[840,1120]{1,0:T(8,128)(2,1)} %bitcast.26) | data formatting | bytes 3763200 | tf_op jit(solution)/shard_map/reshape | solution.py:849
  9.2 3.4 %copy.50 = bf16[1120,1120]{0,1:T(8,128)(2,1)} copy(bf16[1120,1120]{1,0:T(8,128)(2,1)S(1)} %copy-done.3) | data formatting | bytes 5017600 | tf_op args[9]
  19.7 16.1 %front.1 = (bf16[1120,768]{1,0:T(8,128)(2,1)}, bf16[1120,768]{1,0:T(8,128)(2,1)}, bf16[840,768]{1,0:T(8,128)(2,1)}, bf16[2,5,384,384]{3,2,1,0:T(8,128)(2,1)}, bf16[280,768]{1,0:T(8,128)(2,1)}) custom-call(s32[1]{0:T(128)} %bitcast.place_ref, s32[2]{0:T(128)} %length_ref.1, bf16[280,768]{1,0:T(8,128)(2,1)} %bitcast.34, ...), custom_call_target="tpu_custom_call" | custom-call | tf_op jit(solution)/shard_map/front/pallas_call | solution.py:52
  36.7 2.3 copy.57
  39.0 3.4 %copy.55 = bf16[1120,1120]{0,1:T(8,128)(2,1)} copy(bf16[1120,1120]{1,0:T(8,128)(2,1)S(1)} %copy-done.5) | data formatting | bytes 5017600 | tf_op jit(solution)/shard_map/optimization_barrier | solution.py:845
  42.4 2.4 copy.56
  44.8 2.3 copy.58
  51.3 19.9 %middle.1 = (f32[1120,768]{1,0:T(8,128)}, bf16[1120,768]{1,0:T(8,128)(2,1)}, bf16[1120,768]{1,0:T(8,128)(2,1)}, f32[1120,768]{1,0:T(8,128)}) custom-call(bf16[280,768]{1,0:T(8,128)(2,1)S(1)} %copy-done.15, bf16[280,768]{1,0:T(8,128)(2,1)} %collective-permute-done.4.near, bf16[280,768]{1,0:T(8,128)(2,1)} %collective-permute-done.3.far, ...), custom_call_target="tpu_custom_call" | custom-call | tf_op jit(solution)/shard_map/middle/pallas_call | solution.py:52
  73.2 1.8 spread.1
  75.1 2.9 grad.6
  81.3 2.0 copy-done.12
  83.3 9.3 %turn.1 = (bf16[1120,768]{1,0:T(8,128)(2,1)S(1)}, bf16[560,768]{1,0:T(8,128)(2,1)S(1)}, bf16[560,768]{1,0:T(8,128)(2,1)S(1)}, f32[1120,1]{1,0:T(8,128)S(1)}) custom-call(s32[1]{0:T(128)} %bitcast.place_ref, bf16[1120,768]{1,0:T(8,128)(2,1)S(1)} %get-tuple-element.201.refs_1_.cotangent, f32[1120,768]{1,0:T(8,128)S(1)} %copy-done.12, ...), custom_call_target="tpu_custom_call" | custom-call | tf_op jit(solution)/shard_map/turn/pallas_call | solution.py:52
  92.6 2.0 collective-permute-done.12.right
  94.8 2.9 down.3
  99.3 3.5 %collective-permute-start.14 = (bf16[280,1120]{1,0:T(8,128)(2,1)S(1)}, bf16[280,1120]{1,0:T(8,128)(2,1)S(1)}, u32[]{:S(2)}, u32[]{:S(2)}) collective-permute-start(bf16[280,1120]{1,0:T(8,128)(2,1)S(1)} %add.35.left), channel_id=1, source_target_pairs={{0,8},{4,12},{24,16},{28,20},{1,9},{5,13},{25,17},{29,21},{2,10},{... | collective-permute-start | bytes 1881608 | tf_op jit(solution)/shard_map/ppermute | solution.py:775
  102.8 2.8 grad.7
  107.1 2.8 grad.8
  109.9 2.8 grad.9
  112.7 3.9 %collective-permute-done.14.right = bf16[280,1120]{1,0:T(8,128)(2,1)S(1)} collective-permute-done((bf16[280,1120]{1,0:T(8,128)(2,1)S(1)}, bf16[280,1120]{1,0:T(8,128)(2,1)S(1)}, u32[]{:S(2)}, u32[]{:S(2)}) %collective-permute-start.14) | collective-permute-done | bytes 627232 | tf_op jit(solution)/shard_map/ppermute | solution.py:775
  116.5 5.1 %collective-permute-done.15.right = bf16[280,1120]{1,0:T(8,128)(2,1)S(1)} collective-permute-done((bf16[280,1120]{1,0:T(8,128)(2,1)S(1)}, bf16[280,1120]{1,0:T(8,128)(2,1)S(1)}, u32[]{:S(2)}, u32[]{:S(2)}) %collective-permute-start.15) | collective-permute-done | bytes 627232 | tf_op jit(solution)/shard_map/ppermute | solution.py:775
  125.1 4.4 %collective-permute-start.19 = (bf16[280,1120]{1,0:T(8,128)(2,1)S(1)}, bf16[280,1120]{1,0:T(8,128)(2,1)S(1)}, u32[]{:S(2)}, u32[]{:S(2)}) collective-permute-start(bf16[280,1120]{1,0:T(8,128)(2,1)S(1)} %add.38.left), channel_id=1, source_target_pairs={{0,8},{4,12},{24,16},{28,20},{1,9},{5,13},{25,17},{29,21},{2,10},{... | collective-permute-start | bytes 1881608 | tf_op jit(solution)/shard_map/ppermute | solution.py:775
  129.6 16.1 %back.1 = (f32[1120,768]{1,0:T(8,128)S(1)}, bf16[1120,768]{1,0:T(8,128)(2,1)S(1)}, bf16[840,768]{1,0:T(8,128)(2,1)S(1)}, bf16[560,768]{1,0:T(8,128)(2,1)S(1)}, b...) custom-call(s32[1]{0:T(128)} %bitcast.place_ref, bf16[560,768]{1,0:T(8,128)(2,1)S(1)} %add.37.mine, ...), custom_call_target="tpu_custom_call" | custom-call | tf_op jit(solution)/shard_map/back/pallas_call | solution.py:52
  145.7 7.0 %collective-permute-done.20.right = bf16[280,1120]{1,0:T(8,128)(2,1)S(1)} collective-permute-done((bf16[280,1120]{1,0:T(8,128)(2,1)S(1)}, bf16[280,1120]{1,0:T(8,128)(2,1)S(1)}, u32[]{:S(2)}, u32[]{:S(2)}) %collective-permute-start.20) | collective-permute-done | bytes 627232 | tf_op jit(solution)/shard_map/ppermute | solution.py:775
  152.7 2.7 grad.10
  161.2 7.6 %collective-permute-start.27 = (bf16[280,1120]{1,0:T(8,128)(2,1)S(1)}, bf16[280,1120]{1,0:T(8,128)(2,1)S(1)}, u32[]{:S(2)}, u32[]{:S(2)}) collective-permute-start(bf16[280,1120]{1,0:T(8,128)(2,1)S(1)} %add.41.left), channel_id=1, source_target_pairs={{0,8},{4,12},{24,16},{28,20},{1,9},{5,13},{25,17},{29,21},{2,10},{... | collective-permute-start | bytes 1881608 | tf_op jit(solution)/shard_map/ppermute | solution.py:775
  168.8 2.8 grad.11
  171.6 2.1 collective-permute-done.24.right
  173.7 3.7 %collective-permute-done.25.got = bf16[280,1120]{1,0:T(8,128)(2,1)S(1)} collective-permute-done((bf16[280,1120]{1,0:T(8,128)(2,1)S(1)}, bf16[280,1120]{1,0:T(8,128)(2,1)S(1)}, u32[]{:S(2)}, u32[]{:S(2)}) %collective-permute-start.25) | collective-permute-done | bytes 627232 | tf_op jit(solution)/shard_map/ppermute | solution.py:775
  177.4 4.4 %collective-permute-done.27.right = bf16[280,1120]{1,0:T(8,128)(2,1)S(1)} collective-permute-done((bf16[280,1120]{1,0:T(8,128)(2,1)S(1)}, bf16[280,1120]{1,0:T(8,128)(2,1)S(1)}, u32[]{:S(2)}, u32[]{:S(2)}) %collective-permute-start.27) | collective-permute-done | bytes 627232 | tf_op jit(solution)/shard_map/ppermute | solution.py:775
  185.4 6.3 %collective-permute-start.32 = (bf16[280,1120]{1,0:T(8,128)(2,1)S(1)}, bf16[280,1120]{1,0:T(8,128)(2,1)S(1)}, u32[]{:S(2)}, u32[]{:S(2)}) collective-permute-start(bf16[280,1120]{1,0:T(8,128)(2,1)S(1)} %add.45.left), channel_id=1, source_target_pairs={{0,8},{4,12},{24,16},{28,20},{1,9},{5,13},{25,17},{29,21},{2,10},{... | collective-permute-start | bytes 1881608 | tf_op jit(solution)/shard_map/ppermute | solution.py:775
  192.9 6.4 %last.1 = (bf16[280,768]{1,0:T(8,128)(2,1)}, f32[16,1120]{1,0:T(8,128)S(1)}) custom-call(s32[1]{0:T(128)} %bitcast.place_ref, bf16[560,768]{1,0:T(8,128)(2,1)S(1)} %add.44.mine, bf16[560,768]{1,0:T(8,128)(2,1)S(1)} %collective-permute-done.29.other, bf16[1120,768]{1,0:T(8,128)(2,1)S(1)} %copy-done.9, f32[1120,768]{1,0:T(8,128)S(1)} %get-tuple-element.240.dh, ...), custom_call_target="tpu_custom_call" | custom-call | tf_op jit(solution)/shard_map/last/pallas_call | solution.py:52
  199.4 4.0 %collective-permute-done.34.got = bf16[280,768]{1,0:T(8,128)(2,1)S(1)} collective-permute-done((bf16[280,768]{1,0:T(8,128)(2,1)S(1)}, bf16[280,768]{1,0:T(8,128)(2,1)S(1)}, u32[]{:S(2)}, u32[]{:S(2)}) %collective-permute-start.34) | collective-permute-done | bytes 430112 | tf_op jit(solution)/shard_map/ppermute | solution.py:745
  203.4 1.9 collective-permute-done.32.right
  210.1 7.4 %collective-permute-start.35 = (bf16[280,1120]{1,0:T(8,128)(2,1)S(1)}, bf16[280,1120]{1,0:T(8,128)(2,1)S(1)}, u32[]{:S(2)}, u32[]{:S(2)}) collective-permute-start(bf16[280,1120]{1,0:T(8,128)(2,1)S(1)} %add.48.left), channel_id=1, source_target_pairs={{0,8},{4,12},{24,16},{28,20},{1,9},{5,13},{25,17},{29,21},{2,10},{... | collective-permute-start | bytes 1881608 | tf_op jit(solution)/shard_map/ppermute | solution.py:775
  219.0 4.4 %collective-permute-done.39.right = f32[16,1120]{1,0:T(8,128)S(1)} collective-permute-done((f32[16,1120]{1,0:T(8,128)S(1)}, f32[16,1120]{1,0:T(8,128)S(1)}, u32[]{:S(2)}, u32[]{:S(2)}) %collective-permute-start.39) | collective-permute-done | bytes 71712 | tf_op jit(solution)/shard_map/ppermute | solution.py:775
  225.1 4.4 %collective-permute-done.35.right = bf16[280,1120]{1,0:T(8,128)(2,1)S(1)} collective-permute-done((bf16[280,1120]{1,0:T(8,128)(2,1)S(1)}, bf16[280,1120]{1,0:T(8,128)(2,1)S(1)}, u32[]{:S(2)}, u32[]{:S(2)}) %collective-permute-start.35) | collective-permute-done | bytes 627232 | tf_op jit(solution)/shard_map/ppermute | solution.py:775
  233.3 6.3 %collective-permute-start.40 = (bf16[280,1120]{1,0:T(8,128)(2,1)S(1)}, bf16[280,1120]{1,0:T(8,128)(2,1)S(1)}, u32[]{:S(2)}, u32[]{:S(2)}) collective-permute-start(bf16[280,1120]{1,0:T(8,128)(2,1)S(1)} %add.51.left), channel_id=1, source_target_pairs={{0,8},{4,12},{24,16},{28,20},{1,9},{5,13},{25,17},{29,21},{2,10},{... | collective-permute-start | bytes 1881608 | tf_op jit(solution)/shard_map/ppermute | solution.py:775
  240.0 12.2 %collective-permute-done.44.right = f32[16,1120]{1,0:T(8,128)S(1)} collective-permute-done((f32[16,1120]{1,0:T(8,128)S(1)}, f32[16,1120]{1,0:T(8,128)S(1)}, u32[]{:S(2)}, u32[]{:S(2)}) %collective-permute-start.44) | collective-permute-done | bytes 71712 | tf_op jit(solution)/shard_map/ppermute | solution.py:775
  256.8 4.9 %collective-permute-start.48 = (f32[16,1120]{1,0:T(8,128)S(1)}, f32[16,1120]{1,0:T(8,128)S(1)}, u32[]{:S(2)}, u32[]{:S(2)}) collective-permute-start(f32[16,1120]{1,0:T(8,128)S(1)} %add_wide.4.left), channel_id=1, source_target_pairs={{0,8},{4,12},{8,0},{12,4},{16,24},{20,28},{24,16},{28,20},{1,9},{5... | collective-permute-start | bytes 215048 | tf_op jit(solution)/shard_map/ppermute | solution.py:775
  261.7 3.3 %final.3 = f32[1120,1120]{1,0:T(8,128)} custom-call(s32[3]{0:T(128)S(1)} %pad_add_fusion.place_ref.dp_ref, bf16[280,1120]{1,0:T(8,128)(2,1)S(1)} %settle.6.refs_0_, bf16[280,1120]{1,0:T(8,128)(2,1)S(1)} %collective-permute-done.38.refs_1_, bf16[280,1120]{1,0:T(8,128)(2,1)S(1)} %settle.7.refs_2_, bf16[280,1120]{1,0:T(8,128)(2,1)S(1)} %collective-permute-done.43.refs_3_), custom_call_target="tpu_custom_call" | custom-call | tf_op jit(solution)/shard_map/final/pallas_call | solution.py:52
  265.0 5.4 %collective-permute-done.48.right = f32[16,1120]{1,0:T(8,128)S(1)} collective-permute-done((f32[16,1120]{1,0:T(8,128)S(1)}, f32[16,1120]{1,0:T(8,128)S(1)}, u32[]{:S(2)}, u32[]{:S(2)}) %collective-permute-start.48) | collective-permute-done | bytes 71712 | tf_op jit(solution)/shard_map/ppermute | solution.py:775
  275.3 8.8 %collective-permute-done.50.got = bf16[280,1120]{1,0:T(8,128)(2,1)S(1)} collective-permute-done((bf16[280,1120]{1,0:T(8,128)(2,1)S(1)}, bf16[280,1120]{1,0:T(8,128)(2,1)S(1)}, u32[]{:S(2)}, u32[]{:S(2)}) %collective-permute-start.50) | collective-permute-done | bytes 627232 | tf_op jit(solution)/shard_map/ppermute | solution.py:775
  284.1 5.9 %collective-permute-done.49.refs_1_ = bf16[280,1120]{1,0:T(8,128)(2,1)S(1)} collective-permute-done((bf16[280,1120]{1,0:T(8,128)(2,1)S(1)}, bf16[280,1120]{1,0:T(8,128)(2,1)S(1)}, u32[]{:S(2)}, u32[]{:S(2)}) %collective-permute-start.49) | collective-permute-done | bytes 627232 | tf_op jit(solution)/shard_map/ppermute | solution.py:775
  292.5 11.4 %collective-permute-done.51.refs_3_ = bf16[280,1120]{1,0:T(8,128)(2,1)S(1)} collective-permute-done((bf16[280,1120]{1,0:T(8,128)(2,1)S(1)}, bf16[280,1120]{1,0:T(8,128)(2,1)S(1)}, u32[]{:S(2)}, u32[]{:S(2)}) %collective-permute-start.51) | collective-permute-done | bytes 627232 | tf_op jit(solution)/shard_map/ppermute | solution.py:775
  303.8 7.3 %collective-permute-done.52.refs_3_ = bf16[280,1120]{1,0:T(8,128)(2,1)S(1)} collective-permute-done((bf16[280,1120]{1,0:T(8,128)(2,1)S(1)}, bf16[280,1120]{1,0:T(8,128)(2,1)S(1)}, u32[]{:S(2)}, u32[]{:S(2)}) %collective-permute-start.52) | collective-permute-done | bytes 627232 | tf_op jit(solution)/shard_map/ppermute | solution.py:775
  311.1 3.3 %final.4 = f32[1120,1120]{1,0:T(8,128)} custom-call(s32[3]{0:T(128)S(1)} %pad_add_fusion.place_ref.dp_ref, bf16[280,1120]{1,0:T(8,128)(2,1)S(1)} %settle.8.refs_0_, bf16[280,1120]{1,0:T(8,128)(2,1)S(1)} %collective-permute-done.47.refs_1_, bf16[280,1120]{1,0:T(8,128)(2,1)S(1)} %settle.11.refs_2_, bf16[280,1120]{1,0:T(8,128)(2,1)S(1)} %collective-permute-done.52.refs_3_), custom_call_target="tpu_custom_call" | custom-call | tf_op jit(solution)/shard_map/final/pallas_call | solution.py:52
  314.4 3.3 %final.5 = (f32[840,1120]{1,0:T(8,128)}, f32[280,1120]{1,0:T(8,128)}) custom-call(s32[3]{0:T(128)S(1)} %pad_add_fusion.place_ref.dp_ref, bf16[280,1120]{1,0:T(8,128)(2,1)S(1)} %settle.9.refs_0_, bf16[280,1120]{1,0:T(8,128)(2,1)S(1)} %collective-permute-done.49.refs_1_, bf16[280,1120]{1,0:T(8,128)(2,1)S(1)} %settle.10.refs_2_, ...), custom_call_target="tpu_custom_call" | custom-call | tf_op jit(solution)/shard_map/final/pallas_call | solution.py:52
  (187 shorter events, 59.9 us)
Async XLA Ops:
  0.7 13.3 %collective-permute-start = (bf16[280,768]{1,0:T(8,128)(2,1)}, bf16[280,768]{1,0:T(8,128)(2,1)}, u32[]{:S(2)}, u32[]{:S(2)}) collective-permute-start(bf16[280,768]{1,0:T(8,128)(2,1)} %bitcast.32), channel_id=1, source_target_pairs={{0,2},{1,3},{2,0},{3,1},{4,6},{5,7},{6,4},{7,5},{8,10},{9,11},{10,... | collective-permute-start | bytes 1290248 | tf_op jit(solution)/shard_map/ppermute | solution.py:745
  3.7 10.2 %collective-permute-start.1 = (bf16[280,768]{1,0:T(8,128)(2,1)}, bf16[280,768]{1,0:T(8,128)(2,1)}, u32[]{:S(2)}, u32[]{:S(2)}) collective-permute-start(bf16[280,768]{1,0:T(8,128)(2,1)} %bitcast.33), channel_id=1, source_target_pairs={{0,1},{1,0},{2,3},{3,2},{4,5},{5,4},{6,7},{7,6},{8,9},{9,8},{10,11... | collective-permute-start | bytes 1290248 | tf_op jit(solution)/shard_map/ppermute | solution.py:741
  3.7 32.1 %collective-permute-start.6 = (bf16[280,1120]{1,0:T(8,128)(2,1)}, bf16[280,1120]{1,0:T(8,128)(2,1)}, u32[]{:S(2)}, u32[]{:S(2)}) collective-permute-start(bf16[280,1120]{1,0:T(8,128)(2,1)} %out_weight.1), channel_id=1, source_target_pairs={{0,1},{1,0},{2,3},{3,2},{4,5},{5,4},{6,7},{7,6},{8,9},{9,8},{10,11... | collective-permute-start | bytes 1881608 | tf_op jit(solution)/shard_map/ppermute | solution.py:741
  13.9 21.9 %collective-permute-start.5 = (bf16[280,1120]{1,0:T(8,128)(2,1)S(1)}, bf16[280,1120]{1,0:T(8,128)(2,1)}, u32[]{:S(2)}, u32[]{:S(2)}) collective-permute-start(bf16[280,1120]{1,0:T(8,128)(2,1)S(1)} %copy-done.14), channel_id=1, source_target_pairs={{0,2},{1,3},{2,0},{3,1},{4,6},{5,7},{6,4},{7,5},{8,10},{9,11},{10,... | collective-permute-start | bytes 1881608 | tf_op jit(solution)/shard_map/ppermute | solution.py:745
  35.8 9.0 %collective-permute-start.7 = (bf16[280,1120]{1,0:T(8,128)(2,1)}, bf16[280,1120]{1,0:T(8,128)(2,1)}, u32[]{:S(2)}, u32[]{:S(2)}) collective-permute-start(bf16[280,1120]{1,0:T(8,128)(2,1)} %collective-permute-done.5), channel_id=1, source_target_pairs={{0,1},{1,0},{2,3},{3,2},{4,5},{5,4},{6,7},{7,6},{8,9},{9,8},{10,11... | collective-permute-start | bytes 1881608 | tf_op jit(solution)/shard_map/ppermute | solution.py:741
  36.4 12.2 %collective-permute-start.3 = (bf16[280,768]{1,0:T(8,128)(2,1)}, bf16[280,768]{1,0:T(8,128)(2,1)}, u32[]{:S(2)}, u32[]{:S(2)}) collective-permute-start(bf16[280,768]{1,0:T(8,128)(2,1)} %get-tuple-element.180.own.refs_2_), channel_id=1, source_target_pairs={{0,2},{1,3},{2,0},{3,1},{4,6},{5,7},{6,4},{7,5},{8,10},{9,11},{10,... | collective-permute-start | bytes 1290248 | tf_op jit(solution)/shard_map/ppermute | solution.py:745
  36.7 11.9 %collective-permute-start.4 = (bf16[280,768]{1,0:T(8,128)(2,1)}, bf16[280,768]{1,0:T(8,128)(2,1)}, u32[]{:S(2)}, u32[]{:S(2)}) collective-permute-start(bf16[280,768]{1,0:T(8,128)(2,1)} %get-tuple-element.180.own.refs_2_), channel_id=1, source_target_pairs={{0,1},{1,0},{2,3},{3,2},{4,5},{5,4},{6,7},{7,6},{8,9},{9,8},{10,11... | collective-permute-start | bytes 1290248 | tf_op jit(solution)/shard_map/ppermute | solution.py:741
  48.6 22.6 %collective-permute-start.10 = (bf16[280,768]{1,0:T(8,128)(2,1)S(1)}, bf16[280,768]{1,0:T(8,128)(2,1)S(1)}, u32[]{:S(2)}, u32[]{:S(2)}) collective-permute-start(bf16[280,768]{1,0:T(8,128)(2,1)S(1)} %bitcast.22), channel_id=1, source_target_pairs={{0,2},{1,3},{2,0},{3,1},{4,6},{5,7},{6,4},{7,5},{8,10},{9,11},{10,... | collective-permute-start | bytes 1290248 | tf_op jit(solution)/shard_map/ppermute | solution.py:745
  49.3 22.2 %collective-permute-start.9 = (bf16[280,768]{1,0:T(8,128)(2,1)S(1)}, bf16[280,768]{1,0:T(8,128)(2,1)}, u32[]{:S(2)}, u32[]{:S(2)}) collective-permute-start(bf16[280,768]{1,0:T(8,128)(2,1)S(1)} %bitcast.23), channel_id=1, source_target_pairs={{0,1},{1,0},{2,3},{3,2},{4,5},{5,4},{6,7},{7,6},{8,9},{9,8},{10,11... | collective-permute-start | bytes 1290248 | tf_op jit(solution)/shard_map/ppermute | solution.py:741
  78.0 16.6 %collective-permute-start.12 = (bf16[280,1120]{1,0:T(8,128)(2,1)S(1)}, bf16[280,1120]{1,0:T(8,128)(2,1)S(1)}, u32[]{:S(2)}, u32[]{:S(2)}) collective-permute-start(bf16[280,1120]{1,0:T(8,128)(2,1)S(1)} %get-tuple-element.205), channel_id=1, source_target_pairs={{0,4},{4,0},{8,12},{12,8},{16,20},{20,16},{24,28},{28,24},{1,5},{5... | collective-permute-start | bytes 1881608 | tf_op jit(solution)/shard_map/ppermute | solution.py:775
  97.8 18.8 %collective-permute-start.17 = (bf16[560,768]{1,0:T(8,128)(2,1)S(1)}, bf16[560,768]{1,0:T(8,128)(2,1)S(1)}, u32[]{:S(2)}, u32[]{:S(2)}) collective-permute-start(bf16[560,768]{1,0:T(8,128)(2,1)S(1)} %get-tuple-element.218), channel_id=1, source_target_pairs={{0,1},{1,0},{2,3},{3,2},{4,5},{5,4},{6,7},{7,6},{8,9},{9,8},{10,11... | collective-permute-start | bytes 2580488 | tf_op jit(solution)/shard_map/ppermute | solution.py:741
  98.6 23.0 %collective-permute-start.16 = (bf16[560,768]{1,0:T(8,128)(2,1)S(1)}, bf16[560,768]{1,0:T(8,128)(2,1)S(1)}, u32[]{:S(2)}, u32[]{:S(2)}) collective-permute-start(bf16[560,768]{1,0:T(8,128)(2,1)S(1)} %add.36.left), channel_id=1, source_target_pairs={{0,2},{1,3},{2,0},{3,1},{4,6},{5,7},{6,4},{7,5},{8,10},{9,11},{10,... | collective-permute-start | bytes 2580488 | tf_op jit(solution)/shard_map/ppermute | solution.py:745
  99.3 17.3 %collective-permute-start.14 = (bf16[280,1120]{1,0:T(8,128)(2,1)S(1)}, bf16[280,1120]{1,0:T(8,128)(2,1)S(1)}, u32[]{:S(2)}, u32[]{:S(2)}) collective-permute-start(bf16[280,1120]{1,0:T(8,128)(2,1)S(1)} %add.35.left), channel_id=1, source_target_pairs={{0,8},{4,12},{24,16},{28,20},{1,9},{5,13},{25,17},{29,21},{2,10},{... | collective-permute-start | bytes 1881608 | tf_op jit(solution)/shard_map/ppermute | solution.py:775
  105.5 16.1 %collective-permute-start.15 = (bf16[280,1120]{1,0:T(8,128)(2,1)S(1)}, bf16[280,1120]{1,0:T(8,128)(2,1)S(1)}, u32[]{:S(2)}, u32[]{:S(2)}) collective-permute-start(bf16[280,1120]{1,0:T(8,128)(2,1)S(1)} %get-tuple-element.217), channel_id=1, source_target_pairs={{0,4},{4,0},{8,12},{12,8},{16,20},{20,16},{24,28},{28,24},{1,5},{5... | collective-permute-start | bytes 1881608 | tf_op jit(solution)/shard_map/ppermute | solution.py:775
  121.9 7.6 %collective-permute-start.22 = (bf16[560,768]{1,0:T(8,128)(2,1)S(1)}, bf16[560,768]{1,0:T(8,128)(2,1)S(1)}, u32[]{:S(2)}, u32[]{:S(2)}) collective-permute-start(bf16[560,768]{1,0:T(8,128)(2,1)S(1)} %add.37.mine), channel_id=1, source_target_pairs={{0,1},{1,0},{2,3},{3,2},{4,5},{5,4},{6,7},{7,6},{8,9},{9,8},{10,11... | collective-permute-start | bytes 2580488 | tf_op jit(solution)/shard_map/ppermute | solution.py:741
  122.0 23.7 %collective-permute-start.21 = (bf16[280,1120]{1,0:T(8,128)(2,1)S(1)}, bf16[280,1120]{1,0:T(8,128)(2,1)S(1)}, u32[]{:S(2)}, u32[]{:S(2)}) collective-permute-start(bf16[280,1120]{1,0:T(8,128)(2,1)S(1)} %get-tuple-element.231), channel_id=1, source_target_pairs={{0,4},{4,0},{8,12},{12,8},{16,20},{20,16},{24,28},{28,24},{1,5},{5... | collective-permute-start | bytes 1881608 | tf_op jit(solution)/shard_map/ppermute | solution.py:775
  123.6 29.2 %collective-permute-start.20 = (bf16[280,1120]{1,0:T(8,128)(2,1)S(1)}, bf16[280,1120]{1,0:T(8,128)(2,1)S(1)}, u32[]{:S(2)}, u32[]{:S(2)}) collective-permute-start(bf16[280,1120]{1,0:T(8,128)(2,1)S(1)} %get-tuple-element.230), channel_id=1, source_target_pairs={{0,4},{4,0},{8,12},{12,8},{16,20},{20,16},{24,28},{28,24},{1,5},{5... | collective-permute-start | bytes 1881608 | tf_op jit(solution)/shard_map/ppermute | solution.py:775
  124.4 28.3 %collective-permute-start.18 = (bf16[280,1120]{1,0:T(8,128)(2,1)S(1)}, bf16[280,1120]{1,0:T(8,128)(2,1)S(1)}, u32[]{:S(2)}, u32[]{:S(2)}) collective-permute-start(bf16[280,1120]{1,0:T(8,128)(2,1)S(1)} %add.39.left), channel_id=1, source_target_pairs={{8,16},{12,20},{16,8},{20,12},{9,17},{13,21},{17,9},{21,13},{10,18... | collective-permute-start | bytes 1881608 | tf_op jit(solution)/shard_map/ppermute | solution.py:775
  125.1 27.6 %collective-permute-start.19 = (bf16[280,1120]{1,0:T(8,128)(2,1)S(1)}, bf16[280,1120]{1,0:T(8,128)(2,1)S(1)}, u32[]{:S(2)}, u32[]{:S(2)}) collective-permute-start(bf16[280,1120]{1,0:T(8,128)(2,1)S(1)} %add.38.left), channel_id=1, source_target_pairs={{0,8},{4,12},{24,16},{28,20},{1,9},{5,13},{25,17},{29,21},{2,10},{... | collective-permute-start | bytes 1881608 | tf_op jit(solution)/shard_map/ppermute | solution.py:775
  155.8 26.1 %collective-permute-start.28 = (bf16[560,768]{1,0:T(8,128)(2,1)S(1)}, bf16[560,768]{1,0:T(8,128)(2,1)S(1)}, u32[]{:S(2)}, u32[]{:S(2)}) collective-permute-start(bf16[560,768]{1,0:T(8,128)(2,1)S(1)} %add.40.left), channel_id=1, source_target_pairs={{0,2},{1,3},{2,0},{3,1},{4,6},{5,7},{6,4},{7,5},{8,10},{9,11},{10,... | collective-permute-start | bytes 2580488 | tf_op jit(solution)/shard_map/ppermute | solution.py:745
  157.1 16.6 %collective-permute-start.24 = (bf16[280,1120]{1,0:T(8,128)(2,1)S(1)}, bf16[280,1120]{1,0:T(8,128)(2,1)S(1)}, u32[]{:S(2)}, u32[]{:S(2)}) collective-permute-start(bf16[280,1120]{1,0:T(8,128)(2,1)S(1)} %get-tuple-element.250), channel_id=1, source_target_pairs={{0,4},{4,0},{8,12},{12,8},{16,20},{20,16},{24,28},{28,24},{1,5},{5... | collective-permute-start | bytes 1881608 | tf_op jit(solution)/shard_map/ppermute | solution.py:775
  159.2 18.2 %collective-permute-start.25 = (bf16[280,1120]{1,0:T(8,128)(2,1)S(1)}, bf16[280,1120]{1,0:T(8,128)(2,1)S(1)}, u32[]{:S(2)}, u32[]{:S(2)}) collective-permute-start(bf16[280,1120]{1,0:T(8,128)(2,1)S(1)} %add.43.mine), channel_id=1, source_target_pairs={{8,0},{12,4},{16,24},{20,28},{9,1},{13,5},{17,25},{21,29},{10,2},{... | collective-permute-start | bytes 1881608 | tf_op jit(solution)/shard_map/ppermute | solution.py:775
  160.5 17.0 %collective-permute-start.26 = (bf16[280,1120]{1,0:T(8,128)(2,1)S(1)}, bf16[280,1120]{1,0:T(8,128)(2,1)S(1)}, u32[]{:S(2)}, u32[]{:S(2)}) collective-permute-start(bf16[280,1120]{1,0:T(8,128)(2,1)S(1)} %add.42.left), channel_id=1, source_target_pairs={{8,16},{12,20},{16,8},{20,12},{9,17},{13,21},{17,9},{21,13},{10,18... | collective-permute-start | bytes 1881608 | tf_op jit(solution)/shard_map/ppermute | solution.py:775
  161.2 20.7 %collective-permute-start.27 = (bf16[280,1120]{1,0:T(8,128)(2,1)S(1)}, bf16[280,1120]{1,0:T(8,128)(2,1)S(1)}, u32[]{:S(2)}, u32[]{:S(2)}) collective-permute-start(bf16[280,1120]{1,0:T(8,128)(2,1)S(1)} %add.41.left), channel_id=1, source_target_pairs={{0,8},{4,12},{24,16},{28,20},{1,9},{5,13},{25,17},{29,21},{2,10},{... | collective-permute-start | bytes 1881608 | tf_op jit(solution)/shard_map/ppermute | solution.py:775
  182.1 10.0 %collective-permute-start.29 = (bf16[560,768]{1,0:T(8,128)(2,1)S(1)}, bf16[560,768]{1,0:T(8,128)(2,1)S(1)}, u32[]{:S(2)}, u32[]{:S(2)}) collective-permute-start(bf16[560,768]{1,0:T(8,128)(2,1)S(1)} %add.44.mine), channel_id=1, source_target_pairs={{0,1},{1,0},{2,3},{3,2},{4,5},{5,4},{6,7},{7,6},{8,9},{9,8},{10,11... | collective-permute-start | bytes 2580488 | tf_op jit(solution)/shard_map/ppermute | solution.py:741
  182.2 17.2 %collective-permute-start.33 = (bf16[280,1120]{1,0:T(8,128)(2,1)S(1)}, bf16[280,1120]{1,0:T(8,128)(2,1)S(1)}, u32[]{:S(2)}, u32[]{:S(2)}) collective-permute-start(bf16[280,1120]{1,0:T(8,128)(2,1)S(1)} %get-tuple-element.278), channel_id=1, source_target_pairs={{0,4},{4,0},{8,12},{12,8},{16,20},{20,16},{24,28},{28,24},{1,5},{5... | collective-permute-start | bytes 1881608 | tf_op jit(solution)/shard_map/ppermute | solution.py:775
  183.3 20.1 %collective-permute-start.30 = (bf16[280,1120]{1,0:T(8,128)(2,1)S(1)}, bf16[280,1120]{1,0:T(8,128)(2,1)S(1)}, u32[]{:S(2)}, u32[]{:S(2)}) collective-permute-start(bf16[280,1120]{1,0:T(8,128)(2,1)S(1)} %add.47.mine), channel_id=1, source_target_pairs={{8,0},{12,4},{16,24},{20,28},{9,1},{13,5},{17,25},{21,29},{10,2},{... | collective-permute-start | bytes 1881608 | tf_op jit(solution)/shard_map/ppermute | solution.py:775
  184.7 18.7 %collective-permute-start.31 = (bf16[280,1120]{1,0:T(8,128)(2,1)S(1)}, bf16[280,1120]{1,0:T(8,128)(2,1)S(1)}, u32[]{:S(2)}, u32[]{:S(2)}) collective-permute-start(bf16[280,1120]{1,0:T(8,128)(2,1)S(1)} %add.46.left), channel_id=1, source_target_pairs={{8,16},{12,20},{16,8},{20,12},{9,17},{13,21},{17,9},{21,13},{10,18... | collective-permute-start | bytes 1881608 | tf_op jit(solution)/shard_map/ppermute | solution.py:775
  185.4 19.9 %collective-permute-start.32 = (bf16[280,1120]{1,0:T(8,128)(2,1)S(1)}, bf16[280,1120]{1,0:T(8,128)(2,1)S(1)}, u32[]{:S(2)}, u32[]{:S(2)}) collective-permute-start(bf16[280,1120]{1,0:T(8,128)(2,1)S(1)} %add.45.left), channel_id=1, source_target_pairs={{0,8},{4,12},{24,16},{28,20},{1,9},{5,13},{25,17},{29,21},{2,10},{... | collective-permute-start | bytes 1881608 | tf_op jit(solution)/shard_map/ppermute | solution.py:775
  192.1 11.3 %collective-permute-start.34 = (bf16[280,768]{1,0:T(8,128)(2,1)S(1)}, bf16[280,768]{1,0:T(8,128)(2,1)S(1)}, u32[]{:S(2)}, u32[]{:S(2)}) collective-permute-start(bf16[280,768]{1,0:T(8,128)(2,1)S(1)} %get-tuple-element.280), channel_id=1, source_target_pairs={{0,2},{1,3},{2,0},{3,1},{4,6},{5,7},{6,4},{7,5},{8,10},{9,11},{10,... | collective-permute-start | bytes 1290248 | tf_op jit(solution)/shard_map/ppermute | solution.py:745
  206.5 16.9 %collective-permute-start.38 = (bf16[280,1120]{1,0:T(8,128)(2,1)S(1)}, bf16[280,1120]{1,0:T(8,128)(2,1)S(1)}, u32[]{:S(2)}, u32[]{:S(2)}) collective-permute-start(bf16[280,1120]{1,0:T(8,128)(2,1)S(1)} %settle.6.refs_0_), channel_id=1, source_target_pairs={{0,4},{4,0},{8,12},{12,8},{16,20},{20,16},{24,28},{28,24},{1,5},{5... | collective-permute-start | bytes 1881608 | tf_op jit(solution)/shard_map/ppermute | solution.py:775
  208.1 17.0 %collective-permute-start.37 = (bf16[280,1120]{1,0:T(8,128)(2,1)S(1)}, bf16[280,1120]{1,0:T(8,128)(2,1)S(1)}, u32[]{:S(2)}, u32[]{:S(2)}) collective-permute-start(bf16[280,1120]{1,0:T(8,128)(2,1)S(1)} %add.50.mine), channel_id=1, source_target_pairs={{8,0},{12,4},{16,24},{20,28},{9,1},{13,5},{17,25},{21,29},{10,2},{... | collective-permute-start | bytes 1881608 | tf_op jit(solution)/shard_map/ppermute | solution.py:775
  209.4 15.7 %collective-permute-start.36 = (bf16[280,1120]{1,0:T(8,128)(2,1)S(1)}, bf16[280,1120]{1,0:T(8,128)(2,1)S(1)}, u32[]{:S(2)}, u32[]{:S(2)}) collective-permute-start(bf16[280,1120]{1,0:T(8,128)(2,1)S(1)} %add.49.left), channel_id=1, source_target_pairs={{8,16},{12,20},{16,8},{20,12},{9,17},{13,21},{17,9},{21,13},{10,18... | collective-permute-start | bytes 1881608 | tf_op jit(solution)/shard_map/ppermute | solution.py:775
  210.1 19.4 %collective-permute-start.35 = (bf16[280,1120]{1,0:T(8,128)(2,1)S(1)}, bf16[280,1120]{1,0:T(8,128)(2,1)S(1)}, u32[]{:S(2)}, u32[]{:S(2)}) collective-permute-start(bf16[280,1120]{1,0:T(8,128)(2,1)S(1)} %add.48.left), channel_id=1, source_target_pairs={{0,8},{4,12},{24,16},{28,20},{1,9},{5,13},{25,17},{29,21},{2,10},{... | collective-permute-start | bytes 1881608 | tf_op jit(solution)/shard_map/ppermute | solution.py:775
  217.5 5.9 %collective-permute-start.39 = (f32[16,1120]{1,0:T(8,128)S(1)}, f32[16,1120]{1,0:T(8,128)S(1)}, u32[]{:S(2)}, u32[]{:S(2)}) collective-permute-start(f32[16,1120]{1,0:T(8,128)S(1)} %get-tuple-element.291.left), channel_id=1, source_target_pairs={{0,4},{4,0},{8,12},{12,8},{16,20},{20,16},{24,28},{28,24},{1,5},{5... | collective-permute-start | bytes 215048 | tf_op jit(solution)/shard_map/ppermute | solution.py:775
  230.7 21.5 %collective-permute-start.43 = (bf16[280,1120]{1,0:T(8,128)(2,1)S(1)}, bf16[280,1120]{1,0:T(8,128)(2,1)S(1)}, u32[]{:S(2)}, u32[]{:S(2)}) collective-permute-start(bf16[280,1120]{1,0:T(8,128)(2,1)S(1)} %settle.7.refs_2_), channel_id=1, source_target_pairs={{0,4},{4,0},{8,12},{12,8},{16,20},{20,16},{24,28},{28,24},{1,5},{5... | collective-permute-start | bytes 1881608 | tf_op jit(solution)/shard_map/ppermute | solution.py:775
  231.3 20.9 %collective-permute-start.42 = (bf16[280,1120]{1,0:T(8,128)(2,1)S(1)}, bf16[280,1120]{1,0:T(8,128)(2,1)S(1)}, u32[]{:S(2)}, u32[]{:S(2)}) collective-permute-start(bf16[280,1120]{1,0:T(8,128)(2,1)S(1)} %add.53.mine), channel_id=1, source_target_pairs={{8,0},{12,4},{16,24},{20,28},{9,1},{13,5},{17,25},{21,29},{10,2},{... | collective-permute-start | bytes 1881608 | tf_op jit(solution)/shard_map/ppermute | solution.py:775
  232.5 19.6 %collective-permute-start.41 = (bf16[280,1120]{1,0:T(8,128)(2,1)S(1)}, bf16[280,1120]{1,0:T(8,128)(2,1)S(1)}, u32[]{:S(2)}, u32[]{:S(2)}) collective-permute-start(bf16[280,1120]{1,0:T(8,128)(2,1)S(1)} %add.52.left), channel_id=1, source_target_pairs={{8,16},{12,20},{16,8},{20,12},{9,17},{13,21},{17,9},{21,13},{10,18... | collective-permute-start | bytes 1881608 | tf_op jit(solution)/shard_map/ppermute | solution.py:775
  233.3 18.9 %collective-permute-start.40 = (bf16[280,1120]{1,0:T(8,128)(2,1)S(1)}, bf16[280,1120]{1,0:T(8,128)(2,1)S(1)}, u32[]{:S(2)}, u32[]{:S(2)}) collective-permute-start(bf16[280,1120]{1,0:T(8,128)(2,1)S(1)} %add.51.left), channel_id=1, source_target_pairs={{0,8},{4,12},{24,16},{28,20},{1,9},{5,13},{25,17},{29,21},{2,10},{... | collective-permute-start | bytes 1881608 | tf_op jit(solution)/shard_map/ppermute | solution.py:775
  239.5 12.7 %collective-permute-start.44 = (f32[16,1120]{1,0:T(8,128)S(1)}, f32[16,1120]{1,0:T(8,128)S(1)}, u32[]{:S(2)}, u32[]{:S(2)}) collective-permute-start(f32[16,1120]{1,0:T(8,128)S(1)} %add_wide.3.left), channel_id=1, source_target_pairs={{0,16},{4,20},{8,24},{12,28},{16,0},{20,4},{24,8},{28,12},{1,17},{... | collective-permute-start | bytes 215048 | tf_op jit(solution)/shard_map/ppermute | solution.py:775
  253.2 17.2 %collective-permute-start.47 = (bf16[280,1120]{1,0:T(8,128)(2,1)S(1)}, bf16[280,1120]{1,0:T(8,128)(2,1)S(1)}, u32[]{:S(2)}, u32[]{:S(2)}) collective-permute-start(bf16[280,1120]{1,0:T(8,128)(2,1)S(1)} %settle.8.refs_0_), channel_id=1, source_target_pairs={{0,4},{4,0},{8,12},{12,8},{16,20},{20,16},{24,28},{28,24},{1,5},{5... | collective-permute-start | bytes 1881608 | tf_op jit(solution)/shard_map/ppermute | solution.py:775
  254.8 15.6 %collective-permute-start.46 = (bf16[280,1120]{1,0:T(8,128)(2,1)S(1)}, bf16[280,1120]{1,0:T(8,128)(2,1)S(1)}, u32[]{:S(2)}, u32[]{:S(2)}) collective-permute-start(bf16[280,1120]{1,0:T(8,128)(2,1)S(1)} %add.55.mine), channel_id=1, source_target_pairs={{8,0},{12,4},{16,24},{20,28},{9,1},{13,5},{17,25},{21,29},{10,2},{... | collective-permute-start | bytes 1881608 | tf_op jit(solution)/shard_map/ppermute | solution.py:775
  256.1 14.4 %collective-permute-start.45 = (bf16[280,1120]{1,0:T(8,128)(2,1)S(1)}, bf16[280,1120]{1,0:T(8,128)(2,1)S(1)}, u32[]{:S(2)}, u32[]{:S(2)}) collective-permute-start(bf16[280,1120]{1,0:T(8,128)(2,1)S(1)} %add.54.left), channel_id=1, source_target_pairs={{8,16},{12,20},{16,8},{20,12},{9,17},{13,21},{17,9},{21,13},{10,18... | collective-permute-start | bytes 1881608 | tf_op jit(solution)/shard_map/ppermute | solution.py:775
  256.8 13.6 %collective-permute-start.48 = (f32[16,1120]{1,0:T(8,128)S(1)}, f32[16,1120]{1,0:T(8,128)S(1)}, u32[]{:S(2)}, u32[]{:S(2)}) collective-permute-start(f32[16,1120]{1,0:T(8,128)S(1)} %add_wide.4.left), channel_id=1, source_target_pairs={{0,8},{4,12},{8,0},{12,4},{16,24},{20,28},{24,16},{28,20},{1,9},{5... | collective-permute-start | bytes 215048 | tf_op jit(solution)/shard_map/ppermute | solution.py:775
  271.3 12.9 %collective-permute-start.50 = (bf16[280,1120]{1,0:T(8,128)(2,1)S(1)}, bf16[280,1120]{1,0:T(8,128)(2,1)S(1)}, u32[]{:S(2)}, u32[]{:S(2)}) collective-permute-start(bf16[280,1120]{1,0:T(8,128)(2,1)S(1)} %add.56.mine), channel_id=1, source_target_pairs={{8,0},{12,4},{16,24},{20,28},{9,1},{13,5},{17,25},{21,29},{10,2},{... | collective-permute-start | bytes 1881608 | tf_op jit(solution)/shard_map/ppermute | solution.py:775
  272.6 17.4 %collective-permute-start.49 = (bf16[280,1120]{1,0:T(8,128)(2,1)S(1)}, bf16[280,1120]{1,0:T(8,128)(2,1)S(1)}, u32[]{:S(2)}, u32[]{:S(2)}) collective-permute-start(bf16[280,1120]{1,0:T(8,128)(2,1)S(1)} %settle.9.refs_0_), channel_id=1, source_target_pairs={{0,4},{4,0},{8,12},{12,8},{16,20},{20,16},{24,28},{28,24},{1,5},{5... | collective-permute-start | bytes 1881608 | tf_op jit(solution)/shard_map/ppermute | solution.py:775
  273.8 30.1 %collective-permute-start.51 = (bf16[280,1120]{1,0:T(8,128)(2,1)S(1)}, bf16[280,1120]{1,0:T(8,128)(2,1)S(1)}, u32[]{:S(2)}, u32[]{:S(2)}) collective-permute-start(bf16[280,1120]{1,0:T(8,128)(2,1)S(1)} %settle.10.refs_2_), channel_id=1, source_target_pairs={{0,4},{4,0},{8,12},{12,8},{16,20},{20,16},{24,28},{28,24},{1,5},{5... | collective-permute-start | bytes 1881608 | tf_op jit(solution)/shard_map/ppermute | solution.py:775
  290.6 20.5 %collective-permute-start.52 = (bf16[280,1120]{1,0:T(8,128)(2,1)S(1)}, bf16[280,1120]{1,0:T(8,128)(2,1)S(1)}, u32[]{:S(2)}, u32[]{:S(2)}) collective-permute-start(bf16[280,1120]{1,0:T(8,128)(2,1)S(1)} %settle.11.refs_2_), channel_id=1, source_target_pairs={{0,4},{4,0},{8,12},{12,8},{16,20},{20,16},{24,28},{28,24},{1,5},{5... | collective-permute-start | bytes 1881608 | tf_op jit(solution)/shard_map/ppermute | solution.py:775
  (33 other events, 227.9 us)
where the time goes:
time: 319 us; the launch traced here: 318 us
  Pallas kernels  108 us (34%)
  waiting for transfers between devices  101 us (32%)
  starting transfers between devices  77.9 us (24%)
  local copies, waits for them, and re-layouts  28.6 us (9%)
    pallas_call x49, Pallas kernels, call(): pl.pallas_call(kernel, in_specs=[pl.BlockSpec(memory_space=space) for spa...  108 us
    ppermute x33, waiting for transfers between devices, hop(): return lax.ppermute(value, 'dp', pairs)  91.6 us
    ppermute x33, starting transfers between devices, hop(): return lax.ppermute(value, 'dp', pairs)  67.3 us
    optimization_barrier x6, local copies, waits for them, and re-layouts, body(): fence = lambda *values: lax.optimization_barrier(values)  11.3 us
    unnamed x57, local copies, waits for them, and re-layouts  8.72 us
    ppermute x7, starting transfers between devices, swap_chip(): lax.ppermute(value, 'tensor', [(place, place ^ 2) for place in range(4)])  8.63 us
    ppermute x7, waiting for transfers between devices, swap_chip(): lax.ppermute(value, 'tensor', [(place, place ^ 2) for place in range(4)])  6.69 us
  transfers between devices with their start and end apart: 53, of which 22 were waited for; matrix products, arithmetic and copies ran while one was open for 7% of the time, Pallas kernels for 29%

commit v1 on v0

--- a/solution.py
+++ b/solution.py
@@ -902,10 +902,12 @@
     other = swap_core(mine)
     for item in (down_high, down_low, up_low, up_high):
         item.step()
+    down_keep, down_send = down_add_call(place, down_keep, down_got)
+    down_got = swap_chip(down_send)
     dh, low, triple_low, keep, send, back_sums, bias_sums = back_call(
         place, mine, other, resid, grad_rows, columns, output_weight, triple, probs, triple_plain
     )
-    keep, send = end_round([down_low, down_high, up_low, up_high], keep, send)
+    keep, send, down_got = end_round([down_low, down_high, up_low, up_high], keep, send, down_got)
     near = swap_core(send)
     early = cell_sum([(0, 2 * share)], triple_low, first_normed)
     near = add_call(keep, near)
@@ -918,12 +920,10 @@
     other = swap_core(mine)
     for item in (early, up_low, down_high, late):
         item.step()
-    down_keep, down_send = down_add_call(place, down_keep, down_got)
-    down_got = swap_chip(down_send)
     input_grad, small = last_call(
         place, mine, other, rows_all, dh, columns, cotangent_sums, pre_sums, back_sums, bias_sums
     )
-    small, down_got = end_round([down_low, down_high, up_low, up_high, early, late], small, down_got)
+    (small,) = end_round([down_low, down_high, up_low, up_high, early, late], small)
     shifts = (1, 4, 2)
     if groups != 8:
         small = lax.psum(small, "dp")
@@ -932,7 +932,7 @@
         (up_high, late, early, down_high),
         (up_high, late, up_low),
         (early, up_high),
-        (late, up_high),
+        (up_high, late),
     ]
     for place_in, items in enumerate(rounds):
         if groups == 8 and place_in < 3:
@@ -946,7 +946,7 @@
         if groups == 8 and place_in < 3:
             (got,) = end_round(list(items), got)
             small = add_wide_call(small, got)
-        else:
+        elif place_in < 4:
             end_round(list(items))
     up_grad = finish([up_low, up_high], [width])[0]
     triple_grad, output_grad = finish([early, late], [3 * share, share])

time: 319 us -> 315 us (0.987)
  waiting for transfers between devices: 101 us -> 97.5 us
    ppermute x7, waiting for transfers between devices: 6.69 us -> 2.64 us  [swap_chip(): lax.ppermute(value, 'tensor', [(place, place ^ 2) for place in range(4)])]
  transfers between devices with their start and end apart: 53 -> 53, of which waited for: 22 -> 23; matrix products, arithmetic and copies ran while one was open for 7% -> 7% of each run, Pallas kernels for 29% -> 30%
where the time goes in v1:
time: 315 us; the launch traced here: 314 us
  Pallas kernels  108 us (34%)
  waiting for transfers between devices  97.5 us (31%)
  starting transfers between devices  78.6 us (25%)
  local copies, waits for them, and re-layouts  28.6 us (9%)
    pallas_call x49, Pallas kernels, call(): pl.pallas_call(kernel, in_specs=[pl.BlockSpec(memory_space=space) for spa...  108 us
    ppermute x33, waiting for transfers between devices, hop(): return lax.ppermute(value, 'dp', pairs)  91.9 us
    ppermute x33, starting transfers between devices, hop(): return lax.ppermute(value, 'dp', pairs)  67.3 us
    optimization_barrier x6, local copies, waits for them, and re-layouts, body(): fence = lambda *values: lax.optimization_barrier(values)  11.3 us
    ppermute x7, starting transfers between devices, swap_chip(): lax.ppermute(value, 'tensor', [(place, place ^ 2) for place in range(4)])  9.13 us
    unnamed x57, local copies, waits for them, and re-layouts  8.72 us
  transfers between devices with their start and end apart: 53, of which 23 were waited for; matrix products, arithmetic and copies ran while one was open for 7% of the time, Pallas kernels for 30%

profile of v1, /device:TPU:0, one launch (start us, length us, event | category | flops | bytes accessed | tf_op | source)
XLA Modules:
  0.0 314.5 jit_solution(10105120992353021983)
XLA Ops:
  0.7 3.0 collective-permute-start
  5.1 4.0 %copy.51 = bf16[840,1120]{0,1:T(8,128)(2,1)} copy(bf16[840,1120]{1,0:T(8,128)(2,1)} %bitcast.26) | data formatting | bytes 3763200 | tf_op jit(solution)/shard_map/reshape | solution.py:849
  9.2 3.4 %copy.50 = bf16[1120,1120]{0,1:T(8,128)(2,1)} copy(bf16[1120,1120]{1,0:T(8,128)(2,1)S(1)} %copy-done.3) | data formatting | bytes 5017600 | tf_op args[9]
  13.9 1.7 collective-permute-start.5
  19.7 16.1 %front.1 = (bf16[1120,768]{1,0:T(8,128)(2,1)}, bf16[1120,768]{1,0:T(8,128)(2,1)}, bf16[840,768]{1,0:T(8,128)(2,1)}, bf16[2,5,384,384]{3,2,1,0:T(8,128)(2,1)}, bf16[280,768]{1,0:T(8,128)(2,1)}) custom-call(s32[1]{0:T(128)} %bitcast.place_ref, s32[2]{0:T(128)} %length_ref.1, bf16[280,768]{1,0:T(8,128)(2,1)} %bitcast.34, ...), custom_call_target="tpu_custom_call" | custom-call | tf_op jit(solution)/shard_map/front/pallas_call | solution.py:52
  36.7 2.3 copy.57
  39.0 3.4 %copy.55 = bf16[1120,1120]{0,1:T(8,128)(2,1)} copy(bf16[1120,1120]{1,0:T(8,128)(2,1)S(1)} %copy-done.5) | data formatting | bytes 5017600 | tf_op jit(solution)/shard_map/optimization_barrier | solution.py:845
  42.4 2.4 copy.56
  44.8 2.3 copy.58
  51.3 19.9 %middle.1 = (f32[1120,768]{1,0:T(8,128)}, bf16[1120,768]{1,0:T(8,128)(2,1)}, bf16[1120,768]{1,0:T(8,128)(2,1)}, f32[1120,768]{1,0:T(8,128)}) custom-call(bf16[280,768]{1,0:T(8,128)(2,1)S(1)} %copy-done.15, bf16[280,768]{1,0:T(8,128)(2,1)} %collective-permute-done.4.near, bf16[280,768]{1,0:T(8,128)(2,1)} %collective-permute-done.3.far, ...), custom_call_target="tpu_custom_call" | custom-call | tf_op jit(solution)/shard_map/middle/pallas_call | solution.py:52
  73.2 1.8 spread.1
  75.1 2.9 grad.6
  81.3 2.0 copy-done.12
  83.3 9.3 %turn.1 = (bf16[1120,768]{1,0:T(8,128)(2,1)S(1)}, bf16[560,768]{1,0:T(8,128)(2,1)S(1)}, bf16[560,768]{1,0:T(8,128)(2,1)S(1)}, f32[1120,1]{1,0:T(8,128)S(1)}) custom-call(s32[1]{0:T(128)} %bitcast.place_ref, bf16[1120,768]{1,0:T(8,128)(2,1)S(1)} %get-tuple-element.199.refs_1_.cotangent, f32[1120,768]{1,0:T(8,128)S(1)} %copy-done.12, ...), custom_call_target="tpu_custom_call" | custom-call | tf_op jit(solution)/shard_map/turn/pallas_call | solution.py:52
  92.6 2.0 collective-permute-done.12.right
  94.8 3.0 down.3
  99.3 3.5 %collective-permute-start.14 = (bf16[280,1120]{1,0:T(8,128)(2,1)S(1)}, bf16[280,1120]{1,0:T(8,128)(2,1)S(1)}, u32[]{:S(2)}, u32[]{:S(2)}) collective-permute-start(bf16[280,1120]{1,0:T(8,128)(2,1)S(1)} %add.35.left), channel_id=1, source_target_pairs={{0,8},{4,12},{24,16},{28,20},{1,9},{5,13},{25,17},{29,21},{2,10},{... | collective-permute-start | bytes 1881608 | tf_op jit(solution)/shard_map/ppermute | solution.py:775
  102.8 2.7 grad.7
  107.2 2.7 grad.8
  109.9 2.7 grad.9
  112.7 3.9 %collective-permute-done.14.right = bf16[280,1120]{1,0:T(8,128)(2,1)S(1)} collective-permute-done((bf16[280,1120]{1,0:T(8,128)(2,1)S(1)}, bf16[280,1120]{1,0:T(8,128)(2,1)S(1)}, u32[]{:S(2)}, u32[]{:S(2)}) %collective-permute-start.14) | collective-permute-done | bytes 627232 | tf_op jit(solution)/shard_map/ppermute | solution.py:775
  116.6 5.1 %collective-permute-done.15.right = bf16[280,1120]{1,0:T(8,128)(2,1)S(1)} collective-permute-done((bf16[280,1120]{1,0:T(8,128)(2,1)S(1)}, bf16[280,1120]{1,0:T(8,128)(2,1)S(1)}, u32[]{:S(2)}, u32[]{:S(2)}) %collective-permute-start.15) | collective-permute-done | bytes 627232 | tf_op jit(solution)/shard_map/ppermute | solution.py:775
  125.3 4.5 %collective-permute-start.19 = (bf16[280,1120]{1,0:T(8,128)(2,1)S(1)}, bf16[280,1120]{1,0:T(8,128)(2,1)S(1)}, u32[]{:S(2)}, u32[]{:S(2)}) collective-permute-start(bf16[280,1120]{1,0:T(8,128)(2,1)S(1)} %add.38.left), channel_id=1, source_target_pairs={{0,8},{4,12},{24,16},{28,20},{1,9},{5,13},{25,17},{29,21},{2,10},{... | collective-permute-start | bytes 1881608 | tf_op jit(solution)/shard_map/ppermute | solution.py:775
  131.5 16.1 %back.1 = (f32[1120,768]{1,0:T(8,128)S(1)}, bf16[1120,768]{1,0:T(8,128)(2,1)S(1)}, bf16[840,768]{1,0:T(8,128)(2,1)S(1)}, bf16[560,768]{1,0:T(8,128)(2,1)S(1)}, b...) custom-call(s32[1]{0:T(128)} %bitcast.place_ref, bf16[560,768]{1,0:T(8,128)(2,1)S(1)} %add.37.mine, ...), custom_call_target="tpu_custom_call" | custom-call | tf_op jit(solution)/shard_map/back/pallas_call | solution.py:52
  147.6 5.1 %collective-permute-done.20.right = bf16[280,1120]{1,0:T(8,128)(2,1)S(1)} collective-permute-done((bf16[280,1120]{1,0:T(8,128)(2,1)S(1)}, bf16[280,1120]{1,0:T(8,128)(2,1)S(1)}, u32[]{:S(2)}, u32[]{:S(2)}) %collective-permute-start.20) | collective-permute-done | bytes 627232 | tf_op jit(solution)/shard_map/ppermute | solution.py:775
  152.8 2.7 grad.10
  161.5 7.2 %collective-permute-start.28 = (bf16[280,1120]{1,0:T(8,128)(2,1)S(1)}, bf16[280,1120]{1,0:T(8,128)(2,1)S(1)}, u32[]{:S(2)}, u32[]{:S(2)}) collective-permute-start(bf16[280,1120]{1,0:T(8,128)(2,1)S(1)} %add.41.left), channel_id=1, source_target_pairs={{0,8},{4,12},{24,16},{28,20},{1,9},{5,13},{25,17},{29,21},{2,10},{... | collective-permute-start | bytes 1881608 | tf_op jit(solution)/shard_map/ppermute | solution.py:775
  168.7 2.8 grad.11
  171.5 2.3 collective-permute-done.25.right
  173.8 3.7 %collective-permute-done.26.got = bf16[280,1120]{1,0:T(8,128)(2,1)S(1)} collective-permute-done((bf16[280,1120]{1,0:T(8,128)(2,1)S(1)}, bf16[280,1120]{1,0:T(8,128)(2,1)S(1)}, u32[]{:S(2)}, u32[]{:S(2)}) %collective-permute-start.26) | collective-permute-done | bytes 627232 | tf_op jit(solution)/shard_map/ppermute | solution.py:775
  177.5 4.4 %collective-permute-done.28.right = bf16[280,1120]{1,0:T(8,128)(2,1)S(1)} collective-permute-done((bf16[280,1120]{1,0:T(8,128)(2,1)S(1)}, bf16[280,1120]{1,0:T(8,128)(2,1)S(1)}, u32[]{:S(2)}, u32[]{:S(2)}) %collective-permute-start.28) | collective-permute-done | bytes 627232 | tf_op jit(solution)/shard_map/ppermute | solution.py:775
  185.5 6.3 %collective-permute-start.33 = (bf16[280,1120]{1,0:T(8,128)(2,1)S(1)}, bf16[280,1120]{1,0:T(8,128)(2,1)S(1)}, u32[]{:S(2)}, u32[]{:S(2)}) collective-permute-start(bf16[280,1120]{1,0:T(8,128)(2,1)S(1)} %add.45.left), channel_id=1, source_target_pairs={{0,8},{4,12},{24,16},{28,20},{1,9},{5,13},{25,17},{29,21},{2,10},{... | collective-permute-start | bytes 1881608 | tf_op jit(solution)/shard_map/ppermute | solution.py:775
  191.9 6.4 %last.1 = (bf16[280,768]{1,0:T(8,128)(2,1)}, f32[16,1120]{1,0:T(8,128)S(1)}) custom-call(s32[1]{0:T(128)} %bitcast.place_ref, bf16[560,768]{1,0:T(8,128)(2,1)S(1)} %add.44.mine, bf16[560,768]{1,0:T(8,128)(2,1)S(1)} %collective-permute-done.30.other, bf16[1120,768]{1,0:T(8,128)(2,1)S(1)} %copy-done.9, f32[1120,768]{1,0:T(8,128)S(1)} %get-tuple-element.242.dh, ...), custom_call_target="tpu_custom_call" | custom-call | tf_op jit(solution)/shard_map/last/pallas_call | solution.py:52
  199.2 2.9 collective-permute-done.31.got
  202.1 3.4 %collective-permute-done.33.right = bf16[280,1120]{1,0:T(8,128)(2,1)S(1)} collective-permute-done((bf16[280,1120]{1,0:T(8,128)(2,1)S(1)}, bf16[280,1120]{1,0:T(8,128)(2,1)S(1)}, u32[]{:S(2)}, u32[]{:S(2)}) %collective-permute-start.33) | collective-permute-done | bytes 627232 | tf_op jit(solution)/shard_map/ppermute | solution.py:775
  210.2 7.3 %collective-permute-start.35 = (bf16[280,1120]{1,0:T(8,128)(2,1)S(1)}, bf16[280,1120]{1,0:T(8,128)(2,1)S(1)}, u32[]{:S(2)}, u32[]{:S(2)}) collective-permute-start(bf16[280,1120]{1,0:T(8,128)(2,1)S(1)} %add.48.left), channel_id=1, source_target_pairs={{0,8},{4,12},{24,16},{28,20},{1,9},{5,13},{25,17},{29,21},{2,10},{... | collective-permute-start | bytes 1881608 | tf_op jit(solution)/shard_map/ppermute | solution.py:775
  219.0 4.5 %collective-permute-done.39.right = f32[16,1120]{1,0:T(8,128)S(1)} collective-permute-done((f32[16,1120]{1,0:T(8,128)S(1)}, f32[16,1120]{1,0:T(8,128)S(1)}, u32[]{:S(2)}, u32[]{:S(2)}) %collective-permute-start.39) | collective-permute-done | bytes 71712 | tf_op jit(solution)/shard_map/ppermute | solution.py:775
  225.2 4.4 %collective-permute-done.35.right = bf16[280,1120]{1,0:T(8,128)(2,1)S(1)} collective-permute-done((bf16[280,1120]{1,0:T(8,128)(2,1)S(1)}, bf16[280,1120]{1,0:T(8,128)(2,1)S(1)}, u32[]{:S(2)}, u32[]{:S(2)}) %collective-permute-start.35) | collective-permute-done | bytes 627232 | tf_op jit(solution)/shard_map/ppermute | solution.py:775
  233.3 6.3 %collective-permute-start.40 = (bf16[280,1120]{1,0:T(8,128)(2,1)S(1)}, bf16[280,1120]{1,0:T(8,128)(2,1)S(1)}, u32[]{:S(2)}, u32[]{:S(2)}) collective-permute-start(bf16[280,1120]{1,0:T(8,128)(2,1)S(1)} %add.51.left), channel_id=1, source_target_pairs={{0,8},{4,12},{24,16},{28,20},{1,9},{5,13},{25,17},{29,21},{2,10},{... | collective-permute-start | bytes 1881608 | tf_op jit(solution)/shard_map/ppermute | solution.py:775
  240.0 12.2 %collective-permute-done.44.right = f32[16,1120]{1,0:T(8,128)S(1)} collective-permute-done((f32[16,1120]{1,0:T(8,128)S(1)}, f32[16,1120]{1,0:T(8,128)S(1)}, u32[]{:S(2)}, u32[]{:S(2)}) %collective-permute-start.44) | collective-permute-done | bytes 71712 | tf_op jit(solution)/shard_map/ppermute | solution.py:775
  256.8 4.9 %collective-permute-start.48 = (f32[16,1120]{1,0:T(8,128)S(1)}, f32[16,1120]{1,0:T(8,128)S(1)}, u32[]{:S(2)}, u32[]{:S(2)}) collective-permute-start(f32[16,1120]{1,0:T(8,128)S(1)} %add_wide.4.left), channel_id=1, source_target_pairs={{0,8},{4,12},{8,0},{12,4},{16,24},{20,28},{24,16},{28,20},{1,9},{5... | collective-permute-start | bytes 215048 | tf_op jit(solution)/shard_map/ppermute | solution.py:775
  261.8 3.3 %final.3 = f32[1120,1120]{1,0:T(8,128)} custom-call(s32[3]{0:T(128)S(1)} %pad_add_fusion.place_ref.dp_ref, bf16[280,1120]{1,0:T(8,128)(2,1)S(1)} %settle.6.refs_0_, bf16[280,1120]{1,0:T(8,128)(2,1)S(1)} %collective-permute-done.38.refs_1_, bf16[280,1120]{1,0:T(8,128)(2,1)S(1)} %settle.7.refs_2_, bf16[280,1120]{1,0:T(8,128)(2,1)S(1)} %collective-permute-done.43.refs_3_), custom_call_target="tpu_custom_call" | custom-call | tf_op jit(solution)/shard_map/final/pallas_call | solution.py:52
  265.0 5.4 %collective-permute-done.48.right = f32[16,1120]{1,0:T(8,128)S(1)} collective-permute-done((f32[16,1120]{1,0:T(8,128)S(1)}, f32[16,1120]{1,0:T(8,128)S(1)}, u32[]{:S(2)}, u32[]{:S(2)}) %collective-permute-start.48) | collective-permute-done | bytes 71712 | tf_op jit(solution)/shard_map/ppermute | solution.py:775
  273.2 11.0 %collective-permute-done.50.got = bf16[280,1120]{1,0:T(8,128)(2,1)S(1)} collective-permute-done((bf16[280,1120]{1,0:T(8,128)(2,1)S(1)}, bf16[280,1120]{1,0:T(8,128)(2,1)S(1)}, u32[]{:S(2)}, u32[]{:S(2)}) %collective-permute-start.50) | collective-permute-done | bytes 627232 | tf_op jit(solution)/shard_map/ppermute | solution.py:775
  290.6 13.4 %collective-permute-done.51.refs_3_ = bf16[280,1120]{1,0:T(8,128)(2,1)S(1)} collective-permute-done((bf16[280,1120]{1,0:T(8,128)(2,1)S(1)}, bf16[280,1120]{1,0:T(8,128)(2,1)S(1)}, u32[]{:S(2)}, u32[]{:S(2)}) %collective-permute-start.51) | collective-permute-done | bytes 627232 | tf_op jit(solution)/shard_map/ppermute | solution.py:775
  304.0 3.3 %final.4 = f32[1120,1120]{1,0:T(8,128)} custom-call(s32[3]{0:T(128)S(1)} %pad_add_fusion.place_ref.dp_ref, bf16[280,1120]{1,0:T(8,128)(2,1)S(1)} %settle.8.refs_0_, bf16[280,1120]{1,0:T(8,128)(2,1)S(1)} %collective-permute-done.47.refs_1_, bf16[280,1120]{1,0:T(8,128)(2,1)S(1)} %settle.10.refs_2_, bf16[280,1120]{1,0:T(8,128)(2,1)S(1)} %collective-permute-done.51.refs_3_), custom_call_target="tpu_custom_call" | custom-call | tf_op jit(solution)/shard_map/final/pallas_call | solution.py:52
  307.3 3.9 %collective-permute-done.52.refs_3_ = bf16[280,1120]{1,0:T(8,128)(2,1)S(1)} collective-permute-done((bf16[280,1120]{1,0:T(8,128)(2,1)S(1)}, bf16[280,1120]{1,0:T(8,128)(2,1)S(1)}, u32[]{:S(2)}, u32[]{:S(2)}) %collective-permute-start.52) | collective-permute-done | bytes 627232 | tf_op jit(solution)/shard_map/ppermute | solution.py:775
  311.2 3.3 %final.5 = (f32[840,1120]{1,0:T(8,128)}, f32[280,1120]{1,0:T(8,128)}) custom-call(s32[3]{0:T(128)S(1)} %pad_add_fusion.place_ref.dp_ref, bf16[280,1120]{1,0:T(8,128)(2,1)S(1)} %settle.9.refs_0_, bf16[280,1120]{1,0:T(8,128)(2,1)S(1)} %collective-permute-done.49.refs_1_, bf16[280,1120]{1,0:T(8,128)(2,1)S(1)} %settle.11.refs_2_, ...), custom_call_target="tpu_custom_call" | custom-call | tf_op jit(solution)/shard_map/final/pallas_call | solution.py:52
  (187 shorter events, 61.5 us)
Async XLA Ops:
  0.7 13.3 %collective-permute-start = (bf16[280,768]{1,0:T(8,128)(2,1)}, bf16[280,768]{1,0:T(8,128)(2,1)}, u32[]{:S(2)}, u32[]{:S(2)}) collective-permute-start(bf16[280,768]{1,0:T(8,128)(2,1)} %bitcast.32), channel_id=1, source_target_pairs={{0,2},{1,3},{2,0},{3,1},{4,6},{5,7},{6,4},{7,5},{8,10},{9,11},{10,... | collective-permute-start | bytes 1290248 | tf_op jit(solution)/shard_map/ppermute | solution.py:745
  3.7 10.2 %collective-permute-start.1 = (bf16[280,768]{1,0:T(8,128)(2,1)}, bf16[280,768]{1,0:T(8,128)(2,1)}, u32[]{:S(2)}, u32[]{:S(2)}) collective-permute-start(bf16[280,768]{1,0:T(8,128)(2,1)} %bitcast.33), channel_id=1, source_target_pairs={{0,1},{1,0},{2,3},{3,2},{4,5},{5,4},{6,7},{7,6},{8,9},{9,8},{10,11... | collective-permute-start | bytes 1290248 | tf_op jit(solution)/shard_map/ppermute | solution.py:741
  3.7 32.1 %collective-permute-start.6 = (bf16[280,1120]{1,0:T(8,128)(2,1)}, bf16[280,1120]{1,0:T(8,128)(2,1)}, u32[]{:S(2)}, u32[]{:S(2)}) collective-permute-start(bf16[280,1120]{1,0:T(8,128)(2,1)} %out_weight.1), channel_id=1, source_target_pairs={{0,1},{1,0},{2,3},{3,2},{4,5},{5,4},{6,7},{7,6},{8,9},{9,8},{10,11... | collective-permute-start | bytes 1881608 | tf_op jit(solution)/shard_map/ppermute | solution.py:741
  13.9 21.9 %collective-permute-start.5 = (bf16[280,1120]{1,0:T(8,128)(2,1)S(1)}, bf16[280,1120]{1,0:T(8,128)(2,1)}, u32[]{:S(2)}, u32[]{:S(2)}) collective-permute-start(bf16[280,1120]{1,0:T(8,128)(2,1)S(1)} %copy-done.14), channel_id=1, source_target_pairs={{0,2},{1,3},{2,0},{3,1},{4,6},{5,7},{6,4},{7,5},{8,10},{9,11},{10,... | collective-permute-start | bytes 1881608 | tf_op jit(solution)/shard_map/ppermute | solution.py:745
  35.8 9.0 %collective-permute-start.7 = (bf16[280,1120]{1,0:T(8,128)(2,1)}, bf16[280,1120]{1,0:T(8,128)(2,1)}, u32[]{:S(2)}, u32[]{:S(2)}) collective-permute-start(bf16[280,1120]{1,0:T(8,128)(2,1)} %collective-permute-done.5), channel_id=1, source_target_pairs={{0,1},{1,0},{2,3},{3,2},{4,5},{5,4},{6,7},{7,6},{8,9},{9,8},{10,11... | collective-permute-start | bytes 1881608 | tf_op jit(solution)/shard_map/ppermute | solution.py:741
  36.4 12.2 %collective-permute-start.3 = (bf16[280,768]{1,0:T(8,128)(2,1)}, bf16[280,768]{1,0:T(8,128)(2,1)}, u32[]{:S(2)}, u32[]{:S(2)}) collective-permute-start(bf16[280,768]{1,0:T(8,128)(2,1)} %get-tuple-element.178.own.refs_2_), channel_id=1, source_target_pairs={{0,2},{1,3},{2,0},{3,1},{4,6},{5,7},{6,4},{7,5},{8,10},{9,11},{10,... | collective-permute-start | bytes 1290248 | tf_op jit(solution)/shard_map/ppermute | solution.py:745
  36.7 11.9 %collective-permute-start.4 = (bf16[280,768]{1,0:T(8,128)(2,1)}, bf16[280,768]{1,0:T(8,128)(2,1)}, u32[]{:S(2)}, u32[]{:S(2)}) collective-permute-start(bf16[280,768]{1,0:T(8,128)(2,1)} %get-tuple-element.178.own.refs_2_), channel_id=1, source_target_pairs={{0,1},{1,0},{2,3},{3,2},{4,5},{5,4},{6,7},{7,6},{8,9},{9,8},{10,11... | collective-permute-start | bytes 1290248 | tf_op jit(solution)/shard_map/ppermute | solution.py:741
  48.6 22.6 %collective-permute-start.10 = (bf16[280,768]{1,0:T(8,128)(2,1)S(1)}, bf16[280,768]{1,0:T(8,128)(2,1)S(1)}, u32[]{:S(2)}, u32[]{:S(2)}) collective-permute-start(bf16[280,768]{1,0:T(8,128)(2,1)S(1)} %bitcast.22), channel_id=1, source_target_pairs={{0,2},{1,3},{2,0},{3,1},{4,6},{5,7},{6,4},{7,5},{8,10},{9,11},{10,... | collective-permute-start | bytes 1290248 | tf_op jit(solution)/shard_map/ppermute | solution.py:745
  49.3 22.2 %collective-permute-start.9 = (bf16[280,768]{1,0:T(8,128)(2,1)S(1)}, bf16[280,768]{1,0:T(8,128)(2,1)}, u32[]{:S(2)}, u32[]{:S(2)}) collective-permute-start(bf16[280,768]{1,0:T(8,128)(2,1)S(1)} %bitcast.23), channel_id=1, source_target_pairs={{0,1},{1,0},{2,3},{3,2},{4,5},{5,4},{6,7},{7,6},{8,9},{9,8},{10,11... | collective-permute-start | bytes 1290248 | tf_op jit(solution)/shard_map/ppermute | solution.py:741
  78.0 16.6 %collective-permute-start.12 = (bf16[280,1120]{1,0:T(8,128)(2,1)S(1)}, bf16[280,1120]{1,0:T(8,128)(2,1)S(1)}, u32[]{:S(2)}, u32[]{:S(2)}) collective-permute-start(bf16[280,1120]{1,0:T(8,128)(2,1)S(1)} %get-tuple-element.203), channel_id=1, source_target_pairs={{0,4},{4,0},{8,12},{12,8},{16,20},{20,16},{24,28},{28,24},{1,5},{5... | collective-permute-start | bytes 1881608 | tf_op jit(solution)/shard_map/ppermute | solution.py:775
  97.8 18.8 %collective-permute-start.17 = (bf16[560,768]{1,0:T(8,128)(2,1)S(1)}, bf16[560,768]{1,0:T(8,128)(2,1)S(1)}, u32[]{:S(2)}, u32[]{:S(2)}) collective-permute-start(bf16[560,768]{1,0:T(8,128)(2,1)S(1)} %get-tuple-element.216), channel_id=1, source_target_pairs={{0,1},{1,0},{2,3},{3,2},{4,5},{5,4},{6,7},{7,6},{8,9},{9,8},{10,11... | collective-permute-start | bytes 2580488 | tf_op jit(solution)/shard_map/ppermute | solution.py:741
  98.6 23.0 %collective-permute-start.16 = (bf16[560,768]{1,0:T(8,128)(2,1)S(1)}, bf16[560,768]{1,0:T(8,128)(2,1)S(1)}, u32[]{:S(2)}, u32[]{:S(2)}) collective-permute-start(bf16[560,768]{1,0:T(8,128)(2,1)S(1)} %add.36.left), channel_id=1, source_target_pairs={{0,2},{1,3},{2,0},{3,1},{4,6},{5,7},{6,4},{7,5},{8,10},{9,11},{10,... | collective-permute-start | bytes 2580488 | tf_op jit(solution)/shard_map/ppermute | solution.py:745
  99.3 17.3 %collective-permute-start.14 = (bf16[280,1120]{1,0:T(8,128)(2,1)S(1)}, bf16[280,1120]{1,0:T(8,128)(2,1)S(1)}, u32[]{:S(2)}, u32[]{:S(2)}) collective-permute-start(bf16[280,1120]{1,0:T(8,128)(2,1)S(1)} %add.35.left), channel_id=1, source_target_pairs={{0,8},{4,12},{24,16},{28,20},{1,9},{5,13},{25,17},{29,21},{2,10},{... | collective-permute-start | bytes 1881608 | tf_op jit(solution)/shard_map/ppermute | solution.py:775
  105.6 16.1 %collective-permute-start.15 = (bf16[280,1120]{1,0:T(8,128)(2,1)S(1)}, bf16[280,1120]{1,0:T(8,128)(2,1)S(1)}, u32[]{:S(2)}, u32[]{:S(2)}) collective-permute-start(bf16[280,1120]{1,0:T(8,128)(2,1)S(1)} %get-tuple-element.215), channel_id=1, source_target_pairs={{0,4},{4,0},{8,12},{12,8},{16,20},{20,16},{24,28},{28,24},{1,5},{5... | collective-permute-start | bytes 1881608 | tf_op jit(solution)/shard_map/ppermute | solution.py:775
  121.9 8.3 %collective-permute-start.22 = (bf16[560,768]{1,0:T(8,128)(2,1)S(1)}, bf16[560,768]{1,0:T(8,128)(2,1)S(1)}, u32[]{:S(2)}, u32[]{:S(2)}) collective-permute-start(bf16[560,768]{1,0:T(8,128)(2,1)S(1)} %add.37.mine), channel_id=1, source_target_pairs={{0,1},{1,0},{2,3},{3,2},{4,5},{5,4},{6,7},{7,6},{8,9},{9,8},{10,11... | collective-permute-start | bytes 2580488 | tf_op jit(solution)/shard_map/ppermute | solution.py:741
  122.0 25.6 %collective-permute-start.21 = (bf16[280,1120]{1,0:T(8,128)(2,1)S(1)}, bf16[280,1120]{1,0:T(8,128)(2,1)S(1)}, u32[]{:S(2)}, u32[]{:S(2)}) collective-permute-start(bf16[280,1120]{1,0:T(8,128)(2,1)S(1)} %get-tuple-element.232), channel_id=1, source_target_pairs={{0,4},{4,0},{8,12},{12,8},{16,20},{20,16},{24,28},{28,24},{1,5},{5... | collective-permute-start | bytes 1881608 | tf_op jit(solution)/shard_map/ppermute | solution.py:775
  123.6 29.1 %collective-permute-start.20 = (bf16[280,1120]{1,0:T(8,128)(2,1)S(1)}, bf16[280,1120]{1,0:T(8,128)(2,1)S(1)}, u32[]{:S(2)}, u32[]{:S(2)}) collective-permute-start(bf16[280,1120]{1,0:T(8,128)(2,1)S(1)} %get-tuple-element.231), channel_id=1, source_target_pairs={{0,4},{4,0},{8,12},{12,8},{16,20},{20,16},{24,28},{28,24},{1,5},{5... | collective-permute-start | bytes 1881608 | tf_op jit(solution)/shard_map/ppermute | solution.py:775
  124.4 28.3 %collective-permute-start.18 = (bf16[280,1120]{1,0:T(8,128)(2,1)S(1)}, bf16[280,1120]{1,0:T(8,128)(2,1)S(1)}, u32[]{:S(2)}, u32[]{:S(2)}) collective-permute-start(bf16[280,1120]{1,0:T(8,128)(2,1)S(1)} %add.39.left), channel_id=1, source_target_pairs={{8,16},{12,20},{16,8},{20,12},{9,17},{13,21},{17,9},{21,13},{10,18... | collective-permute-start | bytes 1881608 | tf_op jit(solution)/shard_map/ppermute | solution.py:775
  125.3 27.4 %collective-permute-start.19 = (bf16[280,1120]{1,0:T(8,128)(2,1)S(1)}, bf16[280,1120]{1,0:T(8,128)(2,1)S(1)}, u32[]{:S(2)}, u32[]{:S(2)}) collective-permute-start(bf16[280,1120]{1,0:T(8,128)(2,1)S(1)} %add.38.left), channel_id=1, source_target_pairs={{0,8},{4,12},{24,16},{28,20},{1,9},{5,13},{25,17},{29,21},{2,10},{... | collective-permute-start | bytes 1881608 | tf_op jit(solution)/shard_map/ppermute | solution.py:775
  130.2 22.5 %collective-permute-start.23 = (bf16[280,768]{1,0:T(8,128)(2,1)S(1)}, bf16[280,768]{1,0:T(8,128)(2,1)S(1)}, u32[]{:S(2)}, u32[]{:S(2)}) collective-permute-start(bf16[280,768]{1,0:T(8,128)(2,1)S(1)} %get-tuple-element.239), channel_id=1, source_target_pairs={{0,2},{1,3},{2,0},{3,1},{4,6},{5,7},{6,4},{7,5},{8,10},{9,11},{10,... | collective-permute-start | bytes 1290248 | tf_op jit(solution)/shard_map/ppermute | solution.py:745
  155.8 26.1 %collective-permute-start.29 = (bf16[560,768]{1,0:T(8,128)(2,1)S(1)}, bf16[560,768]{1,0:T(8,128)(2,1)S(1)}, u32[]{:S(2)}, u32[]{:S(2)}) collective-permute-start(bf16[560,768]{1,0:T(8,128)(2,1)S(1)} %add.40.left), channel_id=1, source_target_pairs={{0,2},{1,3},{2,0},{3,1},{4,6},{5,7},{6,4},{7,5},{8,10},{9,11},{10,... | collective-permute-start | bytes 2580488 | tf_op jit(solution)/shard_map/ppermute | solution.py:745
  157.2 16.6 %collective-permute-start.25 = (bf16[280,1120]{1,0:T(8,128)(2,1)S(1)}, bf16[280,1120]{1,0:T(8,128)(2,1)S(1)}, u32[]{:S(2)}, u32[]{:S(2)}) collective-permute-start(bf16[280,1120]{1,0:T(8,128)(2,1)S(1)} %get-tuple-element.254), channel_id=1, source_target_pairs={{0,4},{4,0},{8,12},{12,8},{16,20},{20,16},{24,28},{28,24},{1,5},{5... | collective-permute-start | bytes 1881608 | tf_op jit(solution)/shard_map/ppermute | solution.py:775
  159.3 18.2 %collective-permute-start.26 = (bf16[280,1120]{1,0:T(8,128)(2,1)S(1)}, bf16[280,1120]{1,0:T(8,128)(2,1)S(1)}, u32[]{:S(2)}, u32[]{:S(2)}) collective-permute-start(bf16[280,1120]{1,0:T(8,128)(2,1)S(1)} %add.43.mine), channel_id=1, source_target_pairs={{8,0},{12,4},{16,24},{20,28},{9,1},{13,5},{17,25},{21,29},{10,2},{... | collective-permute-start | bytes 1881608 | tf_op jit(solution)/shard_map/ppermute | solution.py:775
  160.6 16.9 %collective-permute-start.27 = (bf16[280,1120]{1,0:T(8,128)(2,1)S(1)}, bf16[280,1120]{1,0:T(8,128)(2,1)S(1)}, u32[]{:S(2)}, u32[]{:S(2)}) collective-permute-start(bf16[280,1120]{1,0:T(8,128)(2,1)S(1)} %add.42.left), channel_id=1, source_target_pairs={{8,16},{12,20},{16,8},{20,12},{9,17},{13,21},{17,9},{21,13},{10,18... | collective-permute-start | bytes 1881608 | tf_op jit(solution)/shard_map/ppermute | solution.py:775
  161.5 20.4 %collective-permute-start.28 = (bf16[280,1120]{1,0:T(8,128)(2,1)S(1)}, bf16[280,1120]{1,0:T(8,128)(2,1)S(1)}, u32[]{:S(2)}, u32[]{:S(2)}) collective-permute-start(bf16[280,1120]{1,0:T(8,128)(2,1)S(1)} %add.41.left), channel_id=1, source_target_pairs={{0,8},{4,12},{24,16},{28,20},{1,9},{5,13},{25,17},{29,21},{2,10},{... | collective-permute-start | bytes 1881608 | tf_op jit(solution)/shard_map/ppermute | solution.py:775
  182.2 9.7 %collective-permute-start.30 = (bf16[560,768]{1,0:T(8,128)(2,1)S(1)}, bf16[560,768]{1,0:T(8,128)(2,1)S(1)}, u32[]{:S(2)}, u32[]{:S(2)}) collective-permute-start(bf16[560,768]{1,0:T(8,128)(2,1)S(1)} %add.44.mine), channel_id=1, source_target_pairs={{0,1},{1,0},{2,3},{3,2},{4,5},{5,4},{6,7},{7,6},{8,9},{9,8},{10,11... | collective-permute-start | bytes 2580488 | tf_op jit(solution)/shard_map/ppermute | solution.py:741
  182.2 16.9 %collective-permute-start.34 = (bf16[280,1120]{1,0:T(8,128)(2,1)S(1)}, bf16[280,1120]{1,0:T(8,128)(2,1)S(1)}, u32[]{:S(2)}, u32[]{:S(2)}) collective-permute-start(bf16[280,1120]{1,0:T(8,128)(2,1)S(1)} %get-tuple-element.277), channel_id=1, source_target_pairs={{0,4},{4,0},{8,12},{12,8},{16,20},{20,16},{24,28},{28,24},{1,5},{5... | collective-permute-start | bytes 1881608 | tf_op jit(solution)/shard_map/ppermute | solution.py:775
  183.4 18.7 %collective-permute-start.31 = (bf16[280,1120]{1,0:T(8,128)(2,1)S(1)}, bf16[280,1120]{1,0:T(8,128)(2,1)S(1)}, u32[]{:S(2)}, u32[]{:S(2)}) collective-permute-start(bf16[280,1120]{1,0:T(8,128)(2,1)S(1)} %add.47.mine), channel_id=1, source_target_pairs={{8,0},{12,4},{16,24},{20,28},{9,1},{13,5},{17,25},{21,29},{10,2},{... | collective-permute-start | bytes 1881608 | tf_op jit(solution)/shard_map/ppermute | solution.py:775
  184.8 17.3 %collective-permute-start.32 = (bf16[280,1120]{1,0:T(8,128)(2,1)S(1)}, bf16[280,1120]{1,0:T(8,128)(2,1)S(1)}, u32[]{:S(2)}, u32[]{:S(2)}) collective-permute-start(bf16[280,1120]{1,0:T(8,128)(2,1)S(1)} %add.46.left), channel_id=1, source_target_pairs={{8,16},{12,20},{16,8},{20,12},{9,17},{13,21},{17,9},{21,13},{10,18... | collective-permute-start | bytes 1881608 | tf_op jit(solution)/shard_map/ppermute | solution.py:775
  185.5 19.9 %collective-permute-start.33 = (bf16[280,1120]{1,0:T(8,128)(2,1)S(1)}, bf16[280,1120]{1,0:T(8,128)(2,1)S(1)}, u32[]{:S(2)}, u32[]{:S(2)}) collective-permute-start(bf16[280,1120]{1,0:T(8,128)(2,1)S(1)} %add.45.left), channel_id=1, source_target_pairs={{0,8},{4,12},{24,16},{28,20},{1,9},{5,13},{25,17},{29,21},{2,10},{... | collective-permute-start | bytes 1881608 | tf_op jit(solution)/shard_map/ppermute | solution.py:775
  206.6 16.9 %collective-permute-start.38 = (bf16[280,1120]{1,0:T(8,128)(2,1)S(1)}, bf16[280,1120]{1,0:T(8,128)(2,1)S(1)}, u32[]{:S(2)}, u32[]{:S(2)}) collective-permute-start(bf16[280,1120]{1,0:T(8,128)(2,1)S(1)} %settle.6.refs_0_), channel_id=1, source_target_pairs={{0,4},{4,0},{8,12},{12,8},{16,20},{20,16},{24,28},{28,24},{1,5},{5... | collective-permute-start | bytes 1881608 | tf_op jit(solution)/shard_map/ppermute | solution.py:775
  208.2 17.0 %collective-permute-start.37 = (bf16[280,1120]{1,0:T(8,128)(2,1)S(1)}, bf16[280,1120]{1,0:T(8,128)(2,1)S(1)}, u32[]{:S(2)}, u32[]{:S(2)}) collective-permute-start(bf16[280,1120]{1,0:T(8,128)(2,1)S(1)} %add.50.mine), channel_id=1, source_target_pairs={{8,0},{12,4},{16,24},{20,28},{9,1},{13,5},{17,25},{21,29},{10,2},{... | collective-permute-start | bytes 1881608 | tf_op jit(solution)/shard_map/ppermute | solution.py:775
  209.5 15.7 %collective-permute-start.36 = (bf16[280,1120]{1,0:T(8,128)(2,1)S(1)}, bf16[280,1120]{1,0:T(8,128)(2,1)S(1)}, u32[]{:S(2)}, u32[]{:S(2)}) collective-permute-start(bf16[280,1120]{1,0:T(8,128)(2,1)S(1)} %add.49.left), channel_id=1, source_target_pairs={{8,16},{12,20},{16,8},{20,12},{9,17},{13,21},{17,9},{21,13},{10,18... | collective-permute-start | bytes 1881608 | tf_op jit(solution)/shard_map/ppermute | solution.py:775
  210.2 19.4 %collective-permute-start.35 = (bf16[280,1120]{1,0:T(8,128)(2,1)S(1)}, bf16[280,1120]{1,0:T(8,128)(2,1)S(1)}, u32[]{:S(2)}, u32[]{:S(2)}) collective-permute-start(bf16[280,1120]{1,0:T(8,128)(2,1)S(1)} %add.48.left), channel_id=1, source_target_pairs={{0,8},{4,12},{24,16},{28,20},{1,9},{5,13},{25,17},{29,21},{2,10},{... | collective-permute-start | bytes 1881608 | tf_op jit(solution)/shard_map/ppermute | solution.py:775
  217.5 6.0 %collective-permute-start.39 = (f32[16,1120]{1,0:T(8,128)S(1)}, f32[16,1120]{1,0:T(8,128)S(1)}, u32[]{:S(2)}, u32[]{:S(2)}) collective-permute-start(f32[16,1120]{1,0:T(8,128)S(1)} %get-tuple-element.289.left), channel_id=1, source_target_pairs={{0,4},{4,0},{8,12},{12,8},{16,20},{20,16},{24,28},{28,24},{1,5},{5... | collective-permute-start | bytes 215048 | tf_op jit(solution)/shard_map/ppermute | solution.py:775
  230.7 21.5 %collective-permute-start.43 = (bf16[280,1120]{1,0:T(8,128)(2,1)S(1)}, bf16[280,1120]{1,0:T(8,128)(2,1)S(1)}, u32[]{:S(2)}, u32[]{:S(2)}) collective-permute-start(bf16[280,1120]{1,0:T(8,128)(2,1)S(1)} %settle.7.refs_2_), channel_id=1, source_target_pairs={{0,4},{4,0},{8,12},{12,8},{16,20},{20,16},{24,28},{28,24},{1,5},{5... | collective-permute-start | bytes 1881608 | tf_op jit(solution)/shard_map/ppermute | solution.py:775
  231.3 20.9 %collective-permute-start.42 = (bf16[280,1120]{1,0:T(8,128)(2,1)S(1)}, bf16[280,1120]{1,0:T(8,128)(2,1)S(1)}, u32[]{:S(2)}, u32[]{:S(2)}) collective-permute-start(bf16[280,1120]{1,0:T(8,128)(2,1)S(1)} %add.53.mine), channel_id=1, source_target_pairs={{8,0},{12,4},{16,24},{20,28},{9,1},{13,5},{17,25},{21,29},{10,2},{... | collective-permute-start | bytes 1881608 | tf_op jit(solution)/shard_map/ppermute | solution.py:775
  232.6 19.6 %collective-permute-start.41 = (bf16[280,1120]{1,0:T(8,128)(2,1)S(1)}, bf16[280,1120]{1,0:T(8,128)(2,1)S(1)}, u32[]{:S(2)}, u32[]{:S(2)}) collective-permute-start(bf16[280,1120]{1,0:T(8,128)(2,1)S(1)} %add.52.left), channel_id=1, source_target_pairs={{8,16},{12,20},{16,8},{20,12},{9,17},{13,21},{17,9},{21,13},{10,18... | collective-permute-start | bytes 1881608 | tf_op jit(solution)/shard_map/ppermute | solution.py:775
  233.3 18.9 %collective-permute-start.40 = (bf16[280,1120]{1,0:T(8,128)(2,1)S(1)}, bf16[280,1120]{1,0:T(8,128)(2,1)S(1)}, u32[]{:S(2)}, u32[]{:S(2)}) collective-permute-start(bf16[280,1120]{1,0:T(8,128)(2,1)S(1)} %add.51.left), channel_id=1, source_target_pairs={{0,8},{4,12},{24,16},{28,20},{1,9},{5,13},{25,17},{29,21},{2,10},{... | collective-permute-start | bytes 1881608 | tf_op jit(solution)/shard_map/ppermute | solution.py:775
  239.6 12.6 %collective-permute-start.44 = (f32[16,1120]{1,0:T(8,128)S(1)}, f32[16,1120]{1,0:T(8,128)S(1)}, u32[]{:S(2)}, u32[]{:S(2)}) collective-permute-start(f32[16,1120]{1,0:T(8,128)S(1)} %add_wide.3.left), channel_id=1, source_target_pairs={{0,16},{4,20},{8,24},{12,28},{16,0},{20,4},{24,8},{28,12},{1,17},{... | collective-permute-start | bytes 215048 | tf_op jit(solution)/shard_map/ppermute | solution.py:775
  253.2 17.2 %collective-permute-start.47 = (bf16[280,1120]{1,0:T(8,128)(2,1)S(1)}, bf16[280,1120]{1,0:T(8,128)(2,1)S(1)}, u32[]{:S(2)}, u32[]{:S(2)}) collective-permute-start(bf16[280,1120]{1,0:T(8,128)(2,1)S(1)} %settle.8.refs_0_), channel_id=1, source_target_pairs={{0,4},{4,0},{8,12},{12,8},{16,20},{20,16},{24,28},{28,24},{1,5},{5... | collective-permute-start | bytes 1881608 | tf_op jit(solution)/shard_map/ppermute | solution.py:775
  254.9 15.6 %collective-permute-start.46 = (bf16[280,1120]{1,0:T(8,128)(2,1)S(1)}, bf16[280,1120]{1,0:T(8,128)(2,1)S(1)}, u32[]{:S(2)}, u32[]{:S(2)}) collective-permute-start(bf16[280,1120]{1,0:T(8,128)(2,1)S(1)} %add.55.mine), channel_id=1, source_target_pairs={{8,0},{12,4},{16,24},{20,28},{9,1},{13,5},{17,25},{21,29},{10,2},{... | collective-permute-start | bytes 1881608 | tf_op jit(solution)/shard_map/ppermute | solution.py:775
  256.1 14.4 %collective-permute-start.45 = (bf16[280,1120]{1,0:T(8,128)(2,1)S(1)}, bf16[280,1120]{1,0:T(8,128)(2,1)S(1)}, u32[]{:S(2)}, u32[]{:S(2)}) collective-permute-start(bf16[280,1120]{1,0:T(8,128)(2,1)S(1)} %add.54.left), channel_id=1, source_target_pairs={{8,16},{12,20},{16,8},{20,12},{9,17},{13,21},{17,9},{21,13},{10,18... | collective-permute-start | bytes 1881608 | tf_op jit(solution)/shard_map/ppermute | solution.py:775
  256.8 13.6 %collective-permute-start.48 = (f32[16,1120]{1,0:T(8,128)S(1)}, f32[16,1120]{1,0:T(8,128)S(1)}, u32[]{:S(2)}, u32[]{:S(2)}) collective-permute-start(f32[16,1120]{1,0:T(8,128)S(1)} %add_wide.4.left), channel_id=1, source_target_pairs={{0,8},{4,12},{8,0},{12,4},{16,24},{20,28},{24,16},{28,20},{1,9},{5... | collective-permute-start | bytes 215048 | tf_op jit(solution)/shard_map/ppermute | solution.py:775
  271.3 12.9 %collective-permute-start.50 = (bf16[280,1120]{1,0:T(8,128)(2,1)S(1)}, bf16[280,1120]{1,0:T(8,128)(2,1)S(1)}, u32[]{:S(2)}, u32[]{:S(2)}) collective-permute-start(bf16[280,1120]{1,0:T(8,128)(2,1)S(1)} %add.56.mine), channel_id=1, source_target_pairs={{8,0},{12,4},{16,24},{20,28},{9,1},{13,5},{17,25},{21,29},{10,2},{... | collective-permute-start | bytes 1881608 | tf_op jit(solution)/shard_map/ppermute | solution.py:775
  272.6 13.3 %collective-permute-start.49 = (bf16[280,1120]{1,0:T(8,128)(2,1)S(1)}, bf16[280,1120]{1,0:T(8,128)(2,1)S(1)}, u32[]{:S(2)}, u32[]{:S(2)}) collective-permute-start(bf16[280,1120]{1,0:T(8,128)(2,1)S(1)} %settle.9.refs_0_), channel_id=1, source_target_pairs={{0,4},{4,0},{8,12},{12,8},{16,20},{20,16},{24,28},{28,24},{1,5},{5... | collective-permute-start | bytes 1881608 | tf_op jit(solution)/shard_map/ppermute | solution.py:775
  286.5 17.4 %collective-permute-start.51 = (bf16[280,1120]{1,0:T(8,128)(2,1)S(1)}, bf16[280,1120]{1,0:T(8,128)(2,1)S(1)}, u32[]{:S(2)}, u32[]{:S(2)}) collective-permute-start(bf16[280,1120]{1,0:T(8,128)(2,1)S(1)} %settle.10.refs_2_), channel_id=1, source_target_pairs={{0,4},{4,0},{8,12},{12,8},{16,20},{20,16},{24,28},{28,24},{1,5},{5... | collective-permute-start | bytes 1881608 | tf_op jit(solution)/shard_map/ppermute | solution.py:775
  287.7 23.5 %collective-permute-start.52 = (bf16[280,1120]{1,0:T(8,128)(2,1)S(1)}, bf16[280,1120]{1,0:T(8,128)(2,1)S(1)}, u32[]{:S(2)}, u32[]{:S(2)}) collective-permute-start(bf16[280,1120]{1,0:T(8,128)(2,1)S(1)} %settle.11.refs_2_), channel_id=1, source_target_pairs={{0,4},{4,0},{8,12},{12,8},{16,20},{20,16},{24,28},{28,24},{1,5},{5... | collective-permute-start | bytes 1881608 | tf_op jit(solution)/shard_map/ppermute | solution.py:775
  (33 other events, 213.0 us)

commit v2 on v1

--- a/solution.py
+++ b/solution.py
@@ -290,7 +290,7 @@
             pltpu.VMEM((width, tokens), bf16),
             pltpu.SemaphoreType.DMA((10 + 2 * (tokens // WIDE),)),
         ],
-        limit=53,
+        limit=50,
         far_in=range(10),
         far_out=range(2),
         transcendentals=tokens * hidden,

time: 315 us -> 314 us (level)
    unnamed x57 -> x53, local copies, waits for them, and re-layouts: 8.72 us -> 7.97 us
where the time goes in v2:
time: 314 us; the launch traced here: 313 us
  Pallas kernels  108 us (34%)
  waiting for transfers between devices  96.9 us (31%)
  starting transfers between devices  79 us (25%)
  local copies, waits for them, and re-layouts  27.2 us (9%)
    pallas_call x49, Pallas kernels, call(): pl.pallas_call(kernel, in_specs=[pl.BlockSpec(memory_space=space) for spa...  108 us
    ppermute x33, waiting for transfers between devices, hop(): return lax.ppermute(value, 'dp', pairs)  90.7 us
    ppermute x33, starting transfers between devices, hop(): return lax.ppermute(value, 'dp', pairs)  67.5 us
    optimization_barrier x6, local copies, waits for them, and re-layouts, body(): fence = lambda *values: lax.optimization_barrier(values)  10.8 us
    ppermute x7, starting transfers between devices, swap_chip(): lax.ppermute(value, 'tensor', [(place, place ^ 2) for place in range(4)])  9.07 us
    unnamed x53, local copies, waits for them, and re-layouts  7.97 us
  transfers between devices with their start and end apart: 53, of which 23 were waited for; matrix products, arithmetic and copies ran while one was open for 7% of the time, Pallas kernels for 30%

profile of v2, /device:TPU:0, one launch (start us, length us, event | category | flops | bytes accessed | tf_op | source)
XLA Modules:
  0.0 313.0 jit_solution(15668089620670269611)
XLA Ops:
  0.7 3.0 collective-permute-start
  5.1 4.0 %copy.51 = bf16[840,1120]{0,1:T(8,128)(2,1)} copy(bf16[840,1120]{1,0:T(8,128)(2,1)} %bitcast.25) | data formatting | bytes 3763200 | tf_op jit(solution)/shard_map/reshape | solution.py:849
  9.2 3.4 %copy.50 = bf16[1120,1120]{0,1:T(8,128)(2,1)} copy(bf16[1120,1120]{1,0:T(8,128)(2,1)S(1)} %copy-done.3) | data formatting | bytes 5017600 | tf_op args[9]
  20.0 16.1 %front.1 = (bf16[1120,768]{1,0:T(8,128)(2,1)}, bf16[1120,768]{1,0:T(8,128)(2,1)}, bf16[840,768]{1,0:T(8,128)(2,1)}, bf16[2,5,384,384]{3,2,1,0:T(8,128)(2,1)}, bf16[280,768]{1,0:T(8,128)(2,1)}) custom-call(s32[1]{0:T(128)} %bitcast.place_ref, s32[2]{0:T(128)} %length_ref.1, bf16[280,768]{1,0:T(8,128)(2,1)} %bitcast.31, bf16[280,768]{1,0:T(8,128)(2,1)} %copy-done.17, ...), custom_call_target="tpu_custom_call" | custom-call | tf_op jit(solution)/shard_map/front/pallas_call | solution.py:52
  37.1 2.3 copy.57
  39.4 3.4 %copy.55 = bf16[1120,1120]{0,1:T(8,128)(2,1)} copy(bf16[1120,1120]{1,0:T(8,128)(2,1)S(1)} %copy-done.5) | data formatting | bytes 5017600 | tf_op jit(solution)/shard_map/optimization_barrier | solution.py:845
  44.4 2.3 copy.58
  46.7 2.1 collective-permute-done.3.far
  50.8 18.5 %middle.1 = (f32[1120,768]{1,0:T(8,128)}, bf16[1120,768]{1,0:T(8,128)(2,1)}, bf16[1120,768]{1,0:T(8,128)(2,1)}, f32[1120,768]{1,0:T(8,128)}) custom-call(bf16[280,768]{1,0:T(8,128)(2,1)S(1)} %copy-done.14, bf16[280,768]{1,0:T(8,128)(2,1)} %collective-permute-done.4.near, bf16[280,768]{1,0:T(8,128)(2,1)} %collective-permute-done.3.far, ...), custom_call_target="tpu_custom_call" | custom-call | tf_op jit(solution)/shard_map/middle/pallas_call | solution.py:52
  69.6 1.8 collective-permute-done.11.both
  71.4 1.9 spread.1
  73.4 2.9 grad.6
  79.6 2.0 copy-done.12
  81.6 9.3 %turn.1 = (bf16[1120,768]{1,0:T(8,128)(2,1)S(1)}, bf16[560,768]{1,0:T(8,128)(2,1)S(1)}, bf16[560,768]{1,0:T(8,128)(2,1)S(1)}, f32[1120,1]{1,0:T(8,128)S(1)}) custom-call(s32[1]{0:T(128)} %bitcast.place_ref, bf16[1120,768]{1,0:T(8,128)(2,1)S(1)} %get-tuple-element.199.refs_1_.cotangent, f32[1120,768]{1,0:T(8,128)S(1)} %copy-done.12, ...), custom_call_target="tpu_custom_call" | custom-call | tf_op jit(solution)/shard_map/turn/pallas_call | solution.py:52
  90.9 2.0 collective-permute-done.12.right
  93.1 2.9 down.3
  97.6 3.5 %collective-permute-start.14 = (bf16[280,1120]{1,0:T(8,128)(2,1)S(1)}, bf16[280,1120]{1,0:T(8,128)(2,1)S(1)}, u32[]{:S(2)}, u32[]{:S(2)}) collective-permute-start(bf16[280,1120]{1,0:T(8,128)(2,1)S(1)} %add.35.left), channel_id=1, source_target_pairs={{0,8},{4,12},{24,16},{28,20},{1,9},{5,13},{25,17},{29,21},{2,10},{... | collective-permute-start | bytes 1881608 | tf_op jit(solution)/shard_map/ppermute | solution.py:775
  101.1 2.8 grad.7
  105.5 2.7 grad.8
  108.2 2.7 grad.9
  111.0 3.9 %collective-permute-done.14.right = bf16[280,1120]{1,0:T(8,128)(2,1)S(1)} collective-permute-done((bf16[280,1120]{1,0:T(8,128)(2,1)S(1)}, bf16[280,1120]{1,0:T(8,128)(2,1)S(1)}, u32[]{:S(2)}, u32[]{:S(2)}) %collective-permute-start.14) | collective-permute-done | bytes 627232 | tf_op jit(solution)/shard_map/ppermute | solution.py:775
  114.9 5.1 %collective-permute-done.15.right = bf16[280,1120]{1,0:T(8,128)(2,1)S(1)} collective-permute-done((bf16[280,1120]{1,0:T(8,128)(2,1)S(1)}, bf16[280,1120]{1,0:T(8,128)(2,1)S(1)}, u32[]{:S(2)}, u32[]{:S(2)}) %collective-permute-start.15) | collective-permute-done | bytes 627232 | tf_op jit(solution)/shard_map/ppermute | solution.py:775
  123.6 4.5 %collective-permute-start.19 = (bf16[280,1120]{1,0:T(8,128)(2,1)S(1)}, bf16[280,1120]{1,0:T(8,128)(2,1)S(1)}, u32[]{:S(2)}, u32[]{:S(2)}) collective-permute-start(bf16[280,1120]{1,0:T(8,128)(2,1)S(1)} %add.38.left), channel_id=1, source_target_pairs={{0,8},{4,12},{24,16},{28,20},{1,9},{5,13},{25,17},{29,21},{2,10},{... | collective-permute-start | bytes 1881608 | tf_op jit(solution)/shard_map/ppermute | solution.py:775
  129.8 17.3 %back.1 = (f32[1120,768]{1,0:T(8,128)S(1)}, bf16[1120,768]{1,0:T(8,128)(2,1)S(1)}, bf16[840,768]{1,0:T(8,128)(2,1)S(1)}, bf16[560,768]{1,0:T(8,128)(2,1)S(1)}, b...) custom-call(s32[1]{0:T(128)} %bitcast.place_ref, bf16[560,768]{1,0:T(8,128)(2,1)S(1)} %add.37.mine, ...), custom_call_target="tpu_custom_call" | custom-call | tf_op jit(solution)/shard_map/back/pallas_call | solution.py:52
  147.2 3.9 %collective-permute-done.20.right = bf16[280,1120]{1,0:T(8,128)(2,1)S(1)} collective-permute-done((bf16[280,1120]{1,0:T(8,128)(2,1)S(1)}, bf16[280,1120]{1,0:T(8,128)(2,1)S(1)}, u32[]{:S(2)}, u32[]{:S(2)}) %collective-permute-start.20) | collective-permute-done | bytes 627232 | tf_op jit(solution)/shard_map/ppermute | solution.py:775
  151.2 2.8 grad.10
  159.8 7.4 %collective-permute-start.28 = (bf16[280,1120]{1,0:T(8,128)(2,1)S(1)}, bf16[280,1120]{1,0:T(8,128)(2,1)S(1)}, u32[]{:S(2)}, u32[]{:S(2)}) collective-permute-start(bf16[280,1120]{1,0:T(8,128)(2,1)S(1)} %add.41.left), channel_id=1, source_target_pairs={{0,8},{4,12},{24,16},{28,20},{1,9},{5,13},{25,17},{29,21},{2,10},{... | collective-permute-start | bytes 1881608 | tf_op jit(solution)/shard_map/ppermute | solution.py:775
  167.2 2.8 grad.11
  170.0 2.1 collective-permute-done.25.right
  172.1 3.7 %collective-permute-done.26.got = bf16[280,1120]{1,0:T(8,128)(2,1)S(1)} collective-permute-done((bf16[280,1120]{1,0:T(8,128)(2,1)S(1)}, bf16[280,1120]{1,0:T(8,128)(2,1)S(1)}, u32[]{:S(2)}, u32[]{:S(2)}) %collective-permute-start.26) | collective-permute-done | bytes 627232 | tf_op jit(solution)/shard_map/ppermute | solution.py:775
  175.8 4.6 %collective-permute-done.28.right = bf16[280,1120]{1,0:T(8,128)(2,1)S(1)} collective-permute-done((bf16[280,1120]{1,0:T(8,128)(2,1)S(1)}, bf16[280,1120]{1,0:T(8,128)(2,1)S(1)}, u32[]{:S(2)}, u32[]{:S(2)}) %collective-permute-start.28) | collective-permute-done | bytes 627232 | tf_op jit(solution)/shard_map/ppermute | solution.py:775
  184.0 6.3 %collective-permute-start.33 = (bf16[280,1120]{1,0:T(8,128)(2,1)S(1)}, bf16[280,1120]{1,0:T(8,128)(2,1)S(1)}, u32[]{:S(2)}, u32[]{:S(2)}) collective-permute-start(bf16[280,1120]{1,0:T(8,128)(2,1)S(1)} %add.45.left), channel_id=1, source_target_pairs={{0,8},{4,12},{24,16},{28,20},{1,9},{5,13},{25,17},{29,21},{2,10},{... | collective-permute-start | bytes 1881608 | tf_op jit(solution)/shard_map/ppermute | solution.py:775
  190.3 6.4 %last.1 = (bf16[280,768]{1,0:T(8,128)(2,1)}, f32[16,1120]{1,0:T(8,128)S(1)}) custom-call(s32[1]{0:T(128)} %bitcast.place_ref, bf16[560,768]{1,0:T(8,128)(2,1)S(1)} %add.44.mine, bf16[560,768]{1,0:T(8,128)(2,1)S(1)} %collective-permute-done.30.other, bf16[1120,768]{1,0:T(8,128)(2,1)S(1)} %copy-done.9, f32[1120,768]{1,0:T(8,128)S(1)} %get-tuple-element.242.dh, ...), custom_call_target="tpu_custom_call" | custom-call | tf_op jit(solution)/shard_map/last/pallas_call | solution.py:52
  197.7 2.9 collective-permute-done.31.got
  200.6 3.3 %collective-permute-done.33.right = bf16[280,1120]{1,0:T(8,128)(2,1)S(1)} collective-permute-done((bf16[280,1120]{1,0:T(8,128)(2,1)S(1)}, bf16[280,1120]{1,0:T(8,128)(2,1)S(1)}, u32[]{:S(2)}, u32[]{:S(2)}) %collective-permute-start.33) | collective-permute-done | bytes 627232 | tf_op jit(solution)/shard_map/ppermute | solution.py:775
  208.6 7.4 %collective-permute-start.35 = (bf16[280,1120]{1,0:T(8,128)(2,1)S(1)}, bf16[280,1120]{1,0:T(8,128)(2,1)S(1)}, u32[]{:S(2)}, u32[]{:S(2)}) collective-permute-start(bf16[280,1120]{1,0:T(8,128)(2,1)S(1)} %add.48.left), channel_id=1, source_target_pairs={{0,8},{4,12},{24,16},{28,20},{1,9},{5,13},{25,17},{29,21},{2,10},{... | collective-permute-start | bytes 1881608 | tf_op jit(solution)/shard_map/ppermute | solution.py:775
  217.6 4.4 %collective-permute-done.39.right = f32[16,1120]{1,0:T(8,128)S(1)} collective-permute-done((f32[16,1120]{1,0:T(8,128)S(1)}, f32[16,1120]{1,0:T(8,128)S(1)}, u32[]{:S(2)}, u32[]{:S(2)}) %collective-permute-start.39) | collective-permute-done | bytes 71712 | tf_op jit(solution)/shard_map/ppermute | solution.py:775
  223.6 4.4 %collective-permute-done.35.right = bf16[280,1120]{1,0:T(8,128)(2,1)S(1)} collective-permute-done((bf16[280,1120]{1,0:T(8,128)(2,1)S(1)}, bf16[280,1120]{1,0:T(8,128)(2,1)S(1)}, u32[]{:S(2)}, u32[]{:S(2)}) %collective-permute-start.35) | collective-permute-done | bytes 627232 | tf_op jit(solution)/shard_map/ppermute | solution.py:775
  231.8 6.3 %collective-permute-start.40 = (bf16[280,1120]{1,0:T(8,128)(2,1)S(1)}, bf16[280,1120]{1,0:T(8,128)(2,1)S(1)}, u32[]{:S(2)}, u32[]{:S(2)}) collective-permute-start(bf16[280,1120]{1,0:T(8,128)(2,1)S(1)} %add.51.left), channel_id=1, source_target_pairs={{0,8},{4,12},{24,16},{28,20},{1,9},{5,13},{25,17},{29,21},{2,10},{... | collective-permute-start | bytes 1881608 | tf_op jit(solution)/shard_map/ppermute | solution.py:775
  238.6 12.2 %collective-permute-done.44.right = f32[16,1120]{1,0:T(8,128)S(1)} collective-permute-done((f32[16,1120]{1,0:T(8,128)S(1)}, f32[16,1120]{1,0:T(8,128)S(1)}, u32[]{:S(2)}, u32[]{:S(2)}) %collective-permute-start.44) | collective-permute-done | bytes 71712 | tf_op jit(solution)/shard_map/ppermute | solution.py:775
  255.3 4.9 %collective-permute-start.48 = (f32[16,1120]{1,0:T(8,128)S(1)}, f32[16,1120]{1,0:T(8,128)S(1)}, u32[]{:S(2)}, u32[]{:S(2)}) collective-permute-start(f32[16,1120]{1,0:T(8,128)S(1)} %add_wide.4.left), channel_id=1, source_target_pairs={{0,8},{4,12},{8,0},{12,4},{16,24},{20,28},{24,16},{28,20},{1,9},{5... | collective-permute-start | bytes 215048 | tf_op jit(solution)/shard_map/ppermute | solution.py:775
  260.2 3.3 %final.3 = f32[1120,1120]{1,0:T(8,128)} custom-call(s32[3]{0:T(128)S(1)} %pad_add_fusion.place_ref.dp_ref, bf16[280,1120]{1,0:T(8,128)(2,1)S(1)} %settle.6.refs_0_, bf16[280,1120]{1,0:T(8,128)(2,1)S(1)} %collective-permute-done.38.refs_1_, bf16[280,1120]{1,0:T(8,128)(2,1)S(1)} %settle.7.refs_2_, bf16[280,1120]{1,0:T(8,128)(2,1)S(1)} %collective-permute-done.43.refs_3_), custom_call_target="tpu_custom_call" | custom-call | tf_op jit(solution)/shard_map/final/pallas_call | solution.py:52
  263.5 5.4 %collective-permute-done.48.right = f32[16,1120]{1,0:T(8,128)S(1)} collective-permute-done((f32[16,1120]{1,0:T(8,128)S(1)}, f32[16,1120]{1,0:T(8,128)S(1)}, u32[]{:S(2)}, u32[]{:S(2)}) %collective-permute-start.48) | collective-permute-done | bytes 71712 | tf_op jit(solution)/shard_map/ppermute | solution.py:775
  271.7 11.0 %collective-permute-done.50.got = bf16[280,1120]{1,0:T(8,128)(2,1)S(1)} collective-permute-done((bf16[280,1120]{1,0:T(8,128)(2,1)S(1)}, bf16[280,1120]{1,0:T(8,128)(2,1)S(1)}, u32[]{:S(2)}, u32[]{:S(2)}) %collective-permute-start.50) | collective-permute-done | bytes 627232 | tf_op jit(solution)/shard_map/ppermute | solution.py:775
  289.1 13.4 %collective-permute-done.51.refs_3_ = bf16[280,1120]{1,0:T(8,128)(2,1)S(1)} collective-permute-done((bf16[280,1120]{1,0:T(8,128)(2,1)S(1)}, bf16[280,1120]{1,0:T(8,128)(2,1)S(1)}, u32[]{:S(2)}, u32[]{:S(2)}) %collective-permute-start.51) | collective-permute-done | bytes 627232 | tf_op jit(solution)/shard_map/ppermute | solution.py:775
  302.5 3.3 %final.4 = f32[1120,1120]{1,0:T(8,128)} custom-call(s32[3]{0:T(128)S(1)} %pad_add_fusion.place_ref.dp_ref, bf16[280,1120]{1,0:T(8,128)(2,1)S(1)} %settle.8.refs_0_, bf16[280,1120]{1,0:T(8,128)(2,1)S(1)} %collective-permute-done.47.refs_1_, bf16[280,1120]{1,0:T(8,128)(2,1)S(1)} %settle.10.refs_2_, bf16[280,1120]{1,0:T(8,128)(2,1)S(1)} %collective-permute-done.51.refs_3_), custom_call_target="tpu_custom_call" | custom-call | tf_op jit(solution)/shard_map/final/pallas_call | solution.py:52
  305.8 3.9 %collective-permute-done.52.refs_3_ = bf16[280,1120]{1,0:T(8,128)(2,1)S(1)} collective-permute-done((bf16[280,1120]{1,0:T(8,128)(2,1)S(1)}, bf16[280,1120]{1,0:T(8,128)(2,1)S(1)}, u32[]{:S(2)}, u32[]{:S(2)}) %collective-permute-start.52) | collective-permute-done | bytes 627232 | tf_op jit(solution)/shard_map/ppermute | solution.py:775
  309.7 3.3 %final.5 = (f32[840,1120]{1,0:T(8,128)}, f32[280,1120]{1,0:T(8,128)}) custom-call(s32[3]{0:T(128)S(1)} %pad_add_fusion.place_ref.dp_ref, bf16[280,1120]{1,0:T(8,128)(2,1)S(1)} %settle.9.refs_0_, bf16[280,1120]{1,0:T(8,128)(2,1)S(1)} %collective-permute-done.49.refs_1_, bf16[280,1120]{1,0:T(8,128)(2,1)S(1)} %settle.11.refs_2_, ...), custom_call_target="tpu_custom_call" | custom-call | tf_op jit(solution)/shard_map/final/pallas_call | solution.py:52
  (183 shorter events, 61.4 us)
Async XLA Ops:
  0.7 13.3 %collective-permute-start = (bf16[280,768]{1,0:T(8,128)(2,1)}, bf16[280,768]{1,0:T(8,128)(2,1)}, u32[]{:S(2)}, u32[]{:S(2)}) collective-permute-start(bf16[280,768]{1,0:T(8,128)(2,1)} %bitcast.29), channel_id=1, source_target_pairs={{0,2},{1,3},{2,0},{3,1},{4,6},{5,7},{6,4},{7,5},{8,10},{9,11},{10,... | collective-permute-start | bytes 1290248 | tf_op jit(solution)/shard_map/ppermute | solution.py:745
  3.7 10.2 %collective-permute-start.1 = (bf16[280,768]{1,0:T(8,128)(2,1)}, bf16[280,768]{1,0:T(8,128)(2,1)S(1)}, u32[]{:S(2)}, u32[]{:S(2)}) collective-permute-start(bf16[280,768]{1,0:T(8,128)(2,1)} %bitcast.30), channel_id=1, source_target_pairs={{0,1},{1,0},{2,3},{3,2},{4,5},{5,4},{6,7},{7,6},{8,9},{9,8},{10,11... | collective-permute-start | bytes 1290248 | tf_op jit(solution)/shard_map/ppermute | solution.py:741
  3.7 32.4 %collective-permute-start.6 = (bf16[280,1120]{1,0:T(8,128)(2,1)}, bf16[280,1120]{1,0:T(8,128)(2,1)}, u32[]{:S(2)}, u32[]{:S(2)}) collective-permute-start(bf16[280,1120]{1,0:T(8,128)(2,1)} %out_weight.1), channel_id=1, source_target_pairs={{0,1},{1,0},{2,3},{3,2},{4,5},{5,4},{6,7},{7,6},{8,9},{9,8},{10,11... | collective-permute-start | bytes 1881608 | tf_op jit(solution)/shard_map/ppermute | solution.py:741
  13.9 22.1 %collective-permute-start.5 = (bf16[280,1120]{1,0:T(8,128)(2,1)}, bf16[280,1120]{1,0:T(8,128)(2,1)}, u32[]{:S(2)}, u32[]{:S(2)}) collective-permute-start(bf16[280,1120]{1,0:T(8,128)(2,1)} %out_weight.1), channel_id=1, source_target_pairs={{0,2},{1,3},{2,0},{3,1},{4,6},{5,7},{6,4},{7,5},{8,10},{9,11},{10,... | collective-permute-start | bytes 1881608 | tf_op jit(solution)/shard_map/ppermute | solution.py:745
  36.1 8.3 %collective-permute-start.7 = (bf16[280,1120]{1,0:T(8,128)(2,1)}, bf16[280,1120]{1,0:T(8,128)(2,1)}, u32[]{:S(2)}, u32[]{:S(2)}) collective-permute-start(bf16[280,1120]{1,0:T(8,128)(2,1)} %collective-permute-done.5), channel_id=1, source_target_pairs={{0,1},{1,0},{2,3},{3,2},{4,5},{5,4},{6,7},{7,6},{8,9},{9,8},{10,11... | collective-permute-start | bytes 1881608 | tf_op jit(solution)/shard_map/ppermute | solution.py:741
  36.6 12.2 %collective-permute-start.3 = (bf16[280,768]{1,0:T(8,128)(2,1)}, bf16[280,768]{1,0:T(8,128)(2,1)}, u32[]{:S(2)}, u32[]{:S(2)}) collective-permute-start(bf16[280,768]{1,0:T(8,128)(2,1)} %get-tuple-element.178.own.refs_2_), channel_id=1, source_target_pairs={{0,2},{1,3},{2,0},{3,1},{4,6},{5,7},{6,4},{7,5},{8,10},{9,11},{10,... | collective-permute-start | bytes 1290248 | tf_op jit(solution)/shard_map/ppermute | solution.py:745
  36.9 11.9 %collective-permute-start.4 = (bf16[280,768]{1,0:T(8,128)(2,1)}, bf16[280,768]{1,0:T(8,128)(2,1)}, u32[]{:S(2)}, u32[]{:S(2)}) collective-permute-start(bf16[280,768]{1,0:T(8,128)(2,1)} %get-tuple-element.178.own.refs_2_), channel_id=1, source_target_pairs={{0,1},{1,0},{2,3},{3,2},{4,5},{5,4},{6,7},{7,6},{8,9},{9,8},{10,11... | collective-permute-start | bytes 1290248 | tf_op jit(solution)/shard_map/ppermute | solution.py:741
  48.8 20.5 %collective-permute-start.10 = (bf16[280,768]{1,0:T(8,128)(2,1)}, bf16[280,768]{1,0:T(8,128)(2,1)}, u32[]{:S(2)}, u32[]{:S(2)}) collective-permute-start(bf16[280,768]{1,0:T(8,128)(2,1)} %bitcast.8.own), channel_id=1, source_target_pairs={{0,2},{1,3},{2,0},{3,1},{4,6},{5,7},{6,4},{7,5},{8,10},{9,11},{10,... | collective-permute-start | bytes 1290248 | tf_op jit(solution)/shard_map/ppermute | solution.py:745
  49.5 20.1 %collective-permute-start.9 = (bf16[280,768]{1,0:T(8,128)(2,1)}, bf16[280,768]{1,0:T(8,128)(2,1)}, u32[]{:S(2)}, u32[]{:S(2)}) collective-permute-start(bf16[280,768]{1,0:T(8,128)(2,1)} %bitcast.8.own), channel_id=1, source_target_pairs={{0,1},{1,0},{2,3},{3,2},{4,5},{5,4},{6,7},{7,6},{8,9},{9,8},{10,11... | collective-permute-start | bytes 1290248 | tf_op jit(solution)/shard_map/ppermute | solution.py:741
  76.3 16.6 %collective-permute-start.12 = (bf16[280,1120]{1,0:T(8,128)(2,1)S(1)}, bf16[280,1120]{1,0:T(8,128)(2,1)S(1)}, u32[]{:S(2)}, u32[]{:S(2)}) collective-permute-start(bf16[280,1120]{1,0:T(8,128)(2,1)S(1)} %get-tuple-element.203), channel_id=1, source_target_pairs={{0,4},{4,0},{8,12},{12,8},{16,20},{20,16},{24,28},{28,24},{1,5},{5... | collective-permute-start | bytes 1881608 | tf_op jit(solution)/shard_map/ppermute | solution.py:775
  96.1 18.8 %collective-permute-start.17 = (bf16[560,768]{1,0:T(8,128)(2,1)S(1)}, bf16[560,768]{1,0:T(8,128)(2,1)S(1)}, u32[]{:S(2)}, u32[]{:S(2)}) collective-permute-start(bf16[560,768]{1,0:T(8,128)(2,1)S(1)} %get-tuple-element.216), channel_id=1, source_target_pairs={{0,1},{1,0},{2,3},{3,2},{4,5},{5,4},{6,7},{7,6},{8,9},{9,8},{10,11... | collective-permute-start | bytes 2580488 | tf_op jit(solution)/shard_map/ppermute | solution.py:741
  96.9 23.1 %collective-permute-start.16 = (bf16[560,768]{1,0:T(8,128)(2,1)S(1)}, bf16[560,768]{1,0:T(8,128)(2,1)S(1)}, u32[]{:S(2)}, u32[]{:S(2)}) collective-permute-start(bf16[560,768]{1,0:T(8,128)(2,1)S(1)} %add.36.left), channel_id=1, source_target_pairs={{0,2},{1,3},{2,0},{3,1},{4,6},{5,7},{6,4},{7,5},{8,10},{9,11},{10,... | collective-permute-start | bytes 2580488 | tf_op jit(solution)/shard_map/ppermute | solution.py:745
  97.6 17.3 %collective-permute-start.14 = (bf16[280,1120]{1,0:T(8,128)(2,1)S(1)}, bf16[280,1120]{1,0:T(8,128)(2,1)S(1)}, u32[]{:S(2)}, u32[]{:S(2)}) collective-permute-start(bf16[280,1120]{1,0:T(8,128)(2,1)S(1)} %add.35.left), channel_id=1, source_target_pairs={{0,8},{4,12},{24,16},{28,20},{1,9},{5,13},{25,17},{29,21},{2,10},{... | collective-permute-start | bytes 1881608 | tf_op jit(solution)/shard_map/ppermute | solution.py:775
  103.9 16.1 %collective-permute-start.15 = (bf16[280,1120]{1,0:T(8,128)(2,1)S(1)}, bf16[280,1120]{1,0:T(8,128)(2,1)S(1)}, u32[]{:S(2)}, u32[]{:S(2)}) collective-permute-start(bf16[280,1120]{1,0:T(8,128)(2,1)S(1)} %get-tuple-element.215), channel_id=1, source_target_pairs={{0,4},{4,0},{8,12},{12,8},{16,20},{20,16},{24,28},{28,24},{1,5},{5... | collective-permute-start | bytes 1881608 | tf_op jit(solution)/shard_map/ppermute | solution.py:775
  120.2 8.3 %collective-permute-start.22 = (bf16[560,768]{1,0:T(8,128)(2,1)S(1)}, bf16[560,768]{1,0:T(8,128)(2,1)S(1)}, u32[]{:S(2)}, u32[]{:S(2)}) collective-permute-start(bf16[560,768]{1,0:T(8,128)(2,1)S(1)} %add.37.mine), channel_id=1, source_target_pairs={{0,1},{1,0},{2,3},{3,2},{4,5},{5,4},{6,7},{7,6},{8,9},{9,8},{10,11... | collective-permute-start | bytes 2580488 | tf_op jit(solution)/shard_map/ppermute | solution.py:741
  120.3 26.8 %collective-permute-start.21 = (bf16[280,1120]{1,0:T(8,128)(2,1)S(1)}, bf16[280,1120]{1,0:T(8,128)(2,1)S(1)}, u32[]{:S(2)}, u32[]{:S(2)}) collective-permute-start(bf16[280,1120]{1,0:T(8,128)(2,1)S(1)} %get-tuple-element.232), channel_id=1, source_target_pairs={{0,4},{4,0},{8,12},{12,8},{16,20},{20,16},{24,28},{28,24},{1,5},{5... | collective-permute-start | bytes 1881608 | tf_op jit(solution)/shard_map/ppermute | solution.py:775
  121.9 29.2 %collective-permute-start.20 = (bf16[280,1120]{1,0:T(8,128)(2,1)S(1)}, bf16[280,1120]{1,0:T(8,128)(2,1)S(1)}, u32[]{:S(2)}, u32[]{:S(2)}) collective-permute-start(bf16[280,1120]{1,0:T(8,128)(2,1)S(1)} %get-tuple-element.231), channel_id=1, source_target_pairs={{0,4},{4,0},{8,12},{12,8},{16,20},{20,16},{24,28},{28,24},{1,5},{5... | collective-permute-start | bytes 1881608 | tf_op jit(solution)/shard_map/ppermute | solution.py:775
  122.8 28.3 %collective-permute-start.18 = (bf16[280,1120]{1,0:T(8,128)(2,1)S(1)}, bf16[280,1120]{1,0:T(8,128)(2,1)S(1)}, u32[]{:S(2)}, u32[]{:S(2)}) collective-permute-start(bf16[280,1120]{1,0:T(8,128)(2,1)S(1)} %add.39.left), channel_id=1, source_target_pairs={{8,16},{12,20},{16,8},{20,12},{9,17},{13,21},{17,9},{21,13},{10,18... | collective-permute-start | bytes 1881608 | tf_op jit(solution)/shard_map/ppermute | solution.py:775
  123.6 27.4 %collective-permute-start.19 = (bf16[280,1120]{1,0:T(8,128)(2,1)S(1)}, bf16[280,1120]{1,0:T(8,128)(2,1)S(1)}, u32[]{:S(2)}, u32[]{:S(2)}) collective-permute-start(bf16[280,1120]{1,0:T(8,128)(2,1)S(1)} %add.38.left), channel_id=1, source_target_pairs={{0,8},{4,12},{24,16},{28,20},{1,9},{5,13},{25,17},{29,21},{2,10},{... | collective-permute-start | bytes 1881608 | tf_op jit(solution)/shard_map/ppermute | solution.py:775
  128.5 22.5 %collective-permute-start.23 = (bf16[280,768]{1,0:T(8,128)(2,1)S(1)}, bf16[280,768]{1,0:T(8,128)(2,1)S(1)}, u32[]{:S(2)}, u32[]{:S(2)}) collective-permute-start(bf16[280,768]{1,0:T(8,128)(2,1)S(1)} %get-tuple-element.239), channel_id=1, source_target_pairs={{0,2},{1,3},{2,0},{3,1},{4,6},{5,7},{6,4},{7,5},{8,10},{9,11},{10,... | collective-permute-start | bytes 1290248 | tf_op jit(solution)/shard_map/ppermute | solution.py:745
  154.2 26.2 %collective-permute-start.29 = (bf16[560,768]{1,0:T(8,128)(2,1)S(1)}, bf16[560,768]{1,0:T(8,128)(2,1)S(1)}, u32[]{:S(2)}, u32[]{:S(2)}) collective-permute-start(bf16[560,768]{1,0:T(8,128)(2,1)S(1)} %add.40.left), channel_id=1, source_target_pairs={{0,2},{1,3},{2,0},{3,1},{4,6},{5,7},{6,4},{7,5},{8,10},{9,11},{10,... | collective-permute-start | bytes 2580488 | tf_op jit(solution)/shard_map/ppermute | solution.py:745
  155.5 16.6 %collective-permute-start.25 = (bf16[280,1120]{1,0:T(8,128)(2,1)S(1)}, bf16[280,1120]{1,0:T(8,128)(2,1)S(1)}, u32[]{:S(2)}, u32[]{:S(2)}) collective-permute-start(bf16[280,1120]{1,0:T(8,128)(2,1)S(1)} %get-tuple-element.254), channel_id=1, source_target_pairs={{0,4},{4,0},{8,12},{12,8},{16,20},{20,16},{24,28},{28,24},{1,5},{5... | collective-permute-start | bytes 1881608 | tf_op jit(solution)/shard_map/ppermute | solution.py:775
  157.5 18.2 %collective-permute-start.26 = (bf16[280,1120]{1,0:T(8,128)(2,1)S(1)}, bf16[280,1120]{1,0:T(8,128)(2,1)S(1)}, u32[]{:S(2)}, u32[]{:S(2)}) collective-permute-start(bf16[280,1120]{1,0:T(8,128)(2,1)S(1)} %add.43.mine), channel_id=1, source_target_pairs={{8,0},{12,4},{16,24},{20,28},{9,1},{13,5},{17,25},{21,29},{10,2},{... | collective-permute-start | bytes 1881608 | tf_op jit(solution)/shard_map/ppermute | solution.py:775
  158.8 16.9 %collective-permute-start.27 = (bf16[280,1120]{1,0:T(8,128)(2,1)S(1)}, bf16[280,1120]{1,0:T(8,128)(2,1)S(1)}, u32[]{:S(2)}, u32[]{:S(2)}) collective-permute-start(bf16[280,1120]{1,0:T(8,128)(2,1)S(1)} %add.42.left), channel_id=1, source_target_pairs={{8,16},{12,20},{16,8},{20,12},{9,17},{13,21},{17,9},{21,13},{10,18... | collective-permute-start | bytes 1881608 | tf_op jit(solution)/shard_map/ppermute | solution.py:775
  159.8 20.6 %collective-permute-start.28 = (bf16[280,1120]{1,0:T(8,128)(2,1)S(1)}, bf16[280,1120]{1,0:T(8,128)(2,1)S(1)}, u32[]{:S(2)}, u32[]{:S(2)}) collective-permute-start(bf16[280,1120]{1,0:T(8,128)(2,1)S(1)} %add.41.left), channel_id=1, source_target_pairs={{0,8},{4,12},{24,16},{28,20},{1,9},{5,13},{25,17},{29,21},{2,10},{... | collective-permute-start | bytes 1881608 | tf_op jit(solution)/shard_map/ppermute | solution.py:775
  180.7 9.7 %collective-permute-start.30 = (bf16[560,768]{1,0:T(8,128)(2,1)S(1)}, bf16[560,768]{1,0:T(8,128)(2,1)S(1)}, u32[]{:S(2)}, u32[]{:S(2)}) collective-permute-start(bf16[560,768]{1,0:T(8,128)(2,1)S(1)} %add.44.mine), channel_id=1, source_target_pairs={{0,1},{1,0},{2,3},{3,2},{4,5},{5,4},{6,7},{7,6},{8,9},{9,8},{10,11... | collective-permute-start | bytes 2580488 | tf_op jit(solution)/shard_map/ppermute | solution.py:741
  180.7 16.9 %collective-permute-start.34 = (bf16[280,1120]{1,0:T(8,128)(2,1)S(1)}, bf16[280,1120]{1,0:T(8,128)(2,1)S(1)}, u32[]{:S(2)}, u32[]{:S(2)}) collective-permute-start(bf16[280,1120]{1,0:T(8,128)(2,1)S(1)} %get-tuple-element.277), channel_id=1, source_target_pairs={{0,4},{4,0},{8,12},{12,8},{16,20},{20,16},{24,28},{28,24},{1,5},{5... | collective-permute-start | bytes 1881608 | tf_op jit(solution)/shard_map/ppermute | solution.py:775
  181.9 18.7 %collective-permute-start.31 = (bf16[280,1120]{1,0:T(8,128)(2,1)S(1)}, bf16[280,1120]{1,0:T(8,128)(2,1)S(1)}, u32[]{:S(2)}, u32[]{:S(2)}) collective-permute-start(bf16[280,1120]{1,0:T(8,128)(2,1)S(1)} %add.47.mine), channel_id=1, source_target_pairs={{8,0},{12,4},{16,24},{20,28},{9,1},{13,5},{17,25},{21,29},{10,2},{... | collective-permute-start | bytes 1881608 | tf_op jit(solution)/shard_map/ppermute | solution.py:775
  183.3 17.3 %collective-permute-start.32 = (bf16[280,1120]{1,0:T(8,128)(2,1)S(1)}, bf16[280,1120]{1,0:T(8,128)(2,1)S(1)}, u32[]{:S(2)}, u32[]{:S(2)}) collective-permute-start(bf16[280,1120]{1,0:T(8,128)(2,1)S(1)} %add.46.left), channel_id=1, source_target_pairs={{8,16},{12,20},{16,8},{20,12},{9,17},{13,21},{17,9},{21,13},{10,18... | collective-permute-start | bytes 1881608 | tf_op jit(solution)/shard_map/ppermute | solution.py:775
  184.0 19.9 %collective-permute-start.33 = (bf16[280,1120]{1,0:T(8,128)(2,1)S(1)}, bf16[280,1120]{1,0:T(8,128)(2,1)S(1)}, u32[]{:S(2)}, u32[]{:S(2)}) collective-permute-start(bf16[280,1120]{1,0:T(8,128)(2,1)S(1)} %add.45.left), channel_id=1, source_target_pairs={{0,8},{4,12},{24,16},{28,20},{1,9},{5,13},{25,17},{29,21},{2,10},{... | collective-permute-start | bytes 1881608 | tf_op jit(solution)/shard_map/ppermute | solution.py:775
  205.1 16.9 %collective-permute-start.38 = (bf16[280,1120]{1,0:T(8,128)(2,1)S(1)}, bf16[280,1120]{1,0:T(8,128)(2,1)S(1)}, u32[]{:S(2)}, u32[]{:S(2)}) collective-permute-start(bf16[280,1120]{1,0:T(8,128)(2,1)S(1)} %settle.6.refs_0_), channel_id=1, source_target_pairs={{0,4},{4,0},{8,12},{12,8},{16,20},{20,16},{24,28},{28,24},{1,5},{5... | collective-permute-start | bytes 1881608 | tf_op jit(solution)/shard_map/ppermute | solution.py:775
  206.6 17.0 %collective-permute-start.37 = (bf16[280,1120]{1,0:T(8,128)(2,1)S(1)}, bf16[280,1120]{1,0:T(8,128)(2,1)S(1)}, u32[]{:S(2)}, u32[]{:S(2)}) collective-permute-start(bf16[280,1120]{1,0:T(8,128)(2,1)S(1)} %add.50.mine), channel_id=1, source_target_pairs={{8,0},{12,4},{16,24},{20,28},{9,1},{13,5},{17,25},{21,29},{10,2},{... | collective-permute-start | bytes 1881608 | tf_op jit(solution)/shard_map/ppermute | solution.py:775
  207.9 15.7 %collective-permute-start.36 = (bf16[280,1120]{1,0:T(8,128)(2,1)S(1)}, bf16[280,1120]{1,0:T(8,128)(2,1)S(1)}, u32[]{:S(2)}, u32[]{:S(2)}) collective-permute-start(bf16[280,1120]{1,0:T(8,128)(2,1)S(1)} %add.49.left), channel_id=1, source_target_pairs={{8,16},{12,20},{16,8},{20,12},{9,17},{13,21},{17,9},{21,13},{10,18... | collective-permute-start | bytes 1881608 | tf_op jit(solution)/shard_map/ppermute | solution.py:775
  208.6 19.4 %collective-permute-start.35 = (bf16[280,1120]{1,0:T(8,128)(2,1)S(1)}, bf16[280,1120]{1,0:T(8,128)(2,1)S(1)}, u32[]{:S(2)}, u32[]{:S(2)}) collective-permute-start(bf16[280,1120]{1,0:T(8,128)(2,1)S(1)} %add.48.left), channel_id=1, source_target_pairs={{0,8},{4,12},{24,16},{28,20},{1,9},{5,13},{25,17},{29,21},{2,10},{... | collective-permute-start | bytes 1881608 | tf_op jit(solution)/shard_map/ppermute | solution.py:775
  216.0 6.0 %collective-permute-start.39 = (f32[16,1120]{1,0:T(8,128)S(1)}, f32[16,1120]{1,0:T(8,128)S(1)}, u32[]{:S(2)}, u32[]{:S(2)}) collective-permute-start(f32[16,1120]{1,0:T(8,128)S(1)} %get-tuple-element.289.left), channel_id=1, source_target_pairs={{0,4},{4,0},{8,12},{12,8},{16,20},{20,16},{24,28},{28,24},{1,5},{5... | collective-permute-start | bytes 215048 | tf_op jit(solution)/shard_map/ppermute | solution.py:775
  229.2 21.5 %collective-permute-start.43 = (bf16[280,1120]{1,0:T(8,128)(2,1)S(1)}, bf16[280,1120]{1,0:T(8,128)(2,1)S(1)}, u32[]{:S(2)}, u32[]{:S(2)}) collective-permute-start(bf16[280,1120]{1,0:T(8,128)(2,1)S(1)} %settle.7.refs_2_), channel_id=1, source_target_pairs={{0,4},{4,0},{8,12},{12,8},{16,20},{20,16},{24,28},{28,24},{1,5},{5... | collective-permute-start | bytes 1881608 | tf_op jit(solution)/shard_map/ppermute | solution.py:775
  229.8 20.9 %collective-permute-start.42 = (bf16[280,1120]{1,0:T(8,128)(2,1)S(1)}, bf16[280,1120]{1,0:T(8,128)(2,1)S(1)}, u32[]{:S(2)}, u32[]{:S(2)}) collective-permute-start(bf16[280,1120]{1,0:T(8,128)(2,1)S(1)} %add.53.mine), channel_id=1, source_target_pairs={{8,0},{12,4},{16,24},{20,28},{9,1},{13,5},{17,25},{21,29},{10,2},{... | collective-permute-start | bytes 1881608 | tf_op jit(solution)/shard_map/ppermute | solution.py:775
  231.1 19.6 %collective-permute-start.41 = (bf16[280,1120]{1,0:T(8,128)(2,1)S(1)}, bf16[280,1120]{1,0:T(8,128)(2,1)S(1)}, u32[]{:S(2)}, u32[]{:S(2)}) collective-permute-start(bf16[280,1120]{1,0:T(8,128)(2,1)S(1)} %add.52.left), channel_id=1, source_target_pairs={{8,16},{12,20},{16,8},{20,12},{9,17},{13,21},{17,9},{21,13},{10,18... | collective-permute-start | bytes 1881608 | tf_op jit(solution)/shard_map/ppermute | solution.py:775
  231.8 18.9 %collective-permute-start.40 = (bf16[280,1120]{1,0:T(8,128)(2,1)S(1)}, bf16[280,1120]{1,0:T(8,128)(2,1)S(1)}, u32[]{:S(2)}, u32[]{:S(2)}) collective-permute-start(bf16[280,1120]{1,0:T(8,128)(2,1)S(1)} %add.51.left), channel_id=1, source_target_pairs={{0,8},{4,12},{24,16},{28,20},{1,9},{5,13},{25,17},{29,21},{2,10},{... | collective-permute-start | bytes 1881608 | tf_op jit(solution)/shard_map/ppermute | solution.py:775
  238.1 12.6 %collective-permute-start.44 = (f32[16,1120]{1,0:T(8,128)S(1)}, f32[16,1120]{1,0:T(8,128)S(1)}, u32[]{:S(2)}, u32[]{:S(2)}) collective-permute-start(f32[16,1120]{1,0:T(8,128)S(1)} %add_wide.3.left), channel_id=1, source_target_pairs={{0,16},{4,20},{8,24},{12,28},{16,0},{20,4},{24,8},{28,12},{1,17},{... | collective-permute-start | bytes 215048 | tf_op jit(solution)/shard_map/ppermute | solution.py:775
  251.8 17.2 %collective-permute-start.47 = (bf16[280,1120]{1,0:T(8,128)(2,1)S(1)}, bf16[280,1120]{1,0:T(8,128)(2,1)S(1)}, u32[]{:S(2)}, u32[]{:S(2)}) collective-permute-start(bf16[280,1120]{1,0:T(8,128)(2,1)S(1)} %settle.8.refs_0_), channel_id=1, source_target_pairs={{0,4},{4,0},{8,12},{12,8},{16,20},{20,16},{24,28},{28,24},{1,5},{5... | collective-permute-start | bytes 1881608 | tf_op jit(solution)/shard_map/ppermute | solution.py:775
  253.3 15.6 %collective-permute-start.46 = (bf16[280,1120]{1,0:T(8,128)(2,1)S(1)}, bf16[280,1120]{1,0:T(8,128)(2,1)S(1)}, u32[]{:S(2)}, u32[]{:S(2)}) collective-permute-start(bf16[280,1120]{1,0:T(8,128)(2,1)S(1)} %add.55.mine), channel_id=1, source_target_pairs={{8,0},{12,4},{16,24},{20,28},{9,1},{13,5},{17,25},{21,29},{10,2},{... | collective-permute-start | bytes 1881608 | tf_op jit(solution)/shard_map/ppermute | solution.py:775
  254.6 14.4 %collective-permute-start.45 = (bf16[280,1120]{1,0:T(8,128)(2,1)S(1)}, bf16[280,1120]{1,0:T(8,128)(2,1)S(1)}, u32[]{:S(2)}, u32[]{:S(2)}) collective-permute-start(bf16[280,1120]{1,0:T(8,128)(2,1)S(1)} %add.54.left), channel_id=1, source_target_pairs={{8,16},{12,20},{16,8},{20,12},{9,17},{13,21},{17,9},{21,13},{10,18... | collective-permute-start | bytes 1881608 | tf_op jit(solution)/shard_map/ppermute | solution.py:775
  255.3 13.6 %collective-permute-start.48 = (f32[16,1120]{1,0:T(8,128)S(1)}, f32[16,1120]{1,0:T(8,128)S(1)}, u32[]{:S(2)}, u32[]{:S(2)}) collective-permute-start(f32[16,1120]{1,0:T(8,128)S(1)} %add_wide.4.left), channel_id=1, source_target_pairs={{0,8},{4,12},{8,0},{12,4},{16,24},{20,28},{24,16},{28,20},{1,9},{5... | collective-permute-start | bytes 215048 | tf_op jit(solution)/shard_map/ppermute | solution.py:775
  269.8 12.9 %collective-permute-start.50 = (bf16[280,1120]{1,0:T(8,128)(2,1)S(1)}, bf16[280,1120]{1,0:T(8,128)(2,1)S(1)}, u32[]{:S(2)}, u32[]{:S(2)}) collective-permute-start(bf16[280,1120]{1,0:T(8,128)(2,1)S(1)} %add.56.mine), channel_id=1, source_target_pairs={{8,0},{12,4},{16,24},{20,28},{9,1},{13,5},{17,25},{21,29},{10,2},{... | collective-permute-start | bytes 1881608 | tf_op jit(solution)/shard_map/ppermute | solution.py:775
  271.1 13.3 %collective-permute-start.49 = (bf16[280,1120]{1,0:T(8,128)(2,1)S(1)}, bf16[280,1120]{1,0:T(8,128)(2,1)S(1)}, u32[]{:S(2)}, u32[]{:S(2)}) collective-permute-start(bf16[280,1120]{1,0:T(8,128)(2,1)S(1)} %settle.9.refs_0_), channel_id=1, source_target_pairs={{0,4},{4,0},{8,12},{12,8},{16,20},{20,16},{24,28},{28,24},{1,5},{5... | collective-permute-start | bytes 1881608 | tf_op jit(solution)/shard_map/ppermute | solution.py:775
  285.0 17.4 %collective-permute-start.51 = (bf16[280,1120]{1,0:T(8,128)(2,1)S(1)}, bf16[280,1120]{1,0:T(8,128)(2,1)S(1)}, u32[]{:S(2)}, u32[]{:S(2)}) collective-permute-start(bf16[280,1120]{1,0:T(8,128)(2,1)S(1)} %settle.10.refs_2_), channel_id=1, source_target_pairs={{0,4},{4,0},{8,12},{12,8},{16,20},{20,16},{24,28},{28,24},{1,5},{5... | collective-permute-start | bytes 1881608 | tf_op jit(solution)/shard_map/ppermute | solution.py:775
  286.2 23.4 %collective-permute-start.52 = (bf16[280,1120]{1,0:T(8,128)(2,1)S(1)}, bf16[280,1120]{1,0:T(8,128)(2,1)S(1)}, u32[]{:S(2)}, u32[]{:S(2)}) collective-permute-start(bf16[280,1120]{1,0:T(8,128)(2,1)S(1)} %settle.11.refs_2_), channel_id=1, source_target_pairs={{0,4},{4,0},{8,12},{12,8},{16,20},{20,16},{24,28},{28,24},{1,5},{5... | collective-permute-start | bytes 1881608 | tf_op jit(solution)/shard_map/ppermute | solution.py:775
  (31 other events, 203.6 us)
